TPU v7x, 32 devices: a whole 2x2x4 slice. The times are simulated.
32 devices in a mesh: dp: 4 (over y, x), dev: 8 (over z, core).
Axes of the slice: x: 2, y: 2, z: 4, core: 2. Of those that a mesh axis runs over, the one named last changes fastest.
Arguments:
- frames: bfloat16 [32, 48, 8192], P(('dp', 'dev')), parts along dimension 0, may hold values from -6 to 6
- clip_ids: int32 [32], P(('dp', 'dev')), parts along dimension 0, may hold values from 0 to 1, never falling along the last dimension, each value on 1 to 7 neighbouring positions
- norm_gain: float32 [2, 64], replicated, may hold values from 0.25 to 1.75
- space_kernel: bfloat16 [2, 3, 3, 64, 64], replicated, may hold values from -0.25 to 0.25
- time_kernel: bfloat16 [2, 5, 64, 64], replicated, may hold values from -0.3125 to 0.3125
Outputs:
- encoded: bfloat16 [32, 48, 8192], P(('dp', 'dev')), parts along dimension 0
There are 4 independent parts, one for each index of `dp`. A program takes and returns all parts, laid end to end along the dimension named above; an argument that names none is the same for every part. Nothing has to cross between parts.
Inputs may be any that keep to these rules, and one draw needn't show every extreme that they name: `clip_ids`: clip ids never fall along the frames; each clip holds 1 to 7 frames, one exactly 7.
All inputs are finite; a program needn't handle non-finite values.
Results may differ from a plain program's by a relative error of at most 0.0061.
Values may be sent and summed in bfloat16 or wider, within the bound.
No kernel may reach another device: no remote copies, remote signals or barrier semaphores. Data moves between devices by JAX's collectives and lax.ppermute only.
A program may use at most 64 MiB of HBM per device.

v0:
```python
import jax
import jax.numpy as jnp
from jax import lax
from jax.sharding import PartitionSpec as P

GROUPS = 32
TIME_TAPS = 5
TIME_DILATION = 2
BLOCKS = 2


def slide_frames(source, frame_offset):
    if frame_offset == 0:
        return source
    blank = jnp.zeros((abs(frame_offset),) + source.shape[1:], source.dtype)
    if frame_offset > 0:
        return jnp.concatenate([source[frame_offset:], blank], 0)
    return jnp.concatenate([blank, source[: source.shape[0] + frame_offset]], 0)


def pair_bands(kernel):
    width = kernel.shape[-1]
    blank = jnp.zeros((width, width), kernel.dtype)
    bands = []
    for r in range(3):
        for d in (-1, 0, 1):
            stacked = []
            for a in (0, 1):
                placed = []
                for b in (0, 1):
                    q = 2 * d + a - b + 1
                    placed.append(kernel[r, q] if 0 <= q <= 2 else blank)
                stacked.append(jnp.concatenate(placed, 1))
            bands.append(jnp.concatenate(stacked, 0))
    return bands


def paired_diagonal(matrix):
    blank = jnp.zeros_like(matrix)
    upper = jnp.concatenate([matrix, blank], 1)
    lower = jnp.concatenate([blank, matrix], 1)
    return jnp.concatenate([upper, lower], 0)


def normed(values, gain):
    local = values.shape[0]
    height = values.shape[1]
    width = gain.shape[0]
    columns = values.shape[2] // width
    per_group = width // GROUPS
    table_entries = height * columns * per_group
    floats = values.astype(jnp.float32)
    summed = jnp.sum(floats, axis=1).reshape(local, columns, GROUPS, per_group).sum(axis=(1, 3))
    center = jnp.tile(jnp.repeat(summed / table_entries, per_group, axis=1), (1, columns))
    shifted = floats - center[:, None, :]
    squares = (
        jnp.sum(shifted * shifted, axis=1)
        .reshape(local, columns, GROUPS, per_group)
        .sum(axis=(1, 3))
    )
    scale = jnp.tile(
        jnp.repeat(lax.rsqrt(squares / table_entries + 1e-06), per_group, axis=1), (1, columns)
    )
    gains = jnp.tile(gain, columns)
    return jax.nn.silu(shifted * scale[:, None, :] * gains).astype(jnp.bfloat16)


def spatial_convolve(act, bands, width):
    local = act.shape[0]
    height = act.shape[1]
    halves = act.shape[2] // (2 * width)
    paired = act.reshape(local, height, halves, 2 * width)
    padded = jnp.pad(paired, ((0, 0), (1, 1), (1, 1), (0, 0)))
    total = jnp.zeros((local * height * halves, 2 * width), jnp.float32)
    for r in range(3):
        for d in (-1, 0, 1):
            window = padded[:, r : r + height, d + 1 : d + 1 + halves, :].reshape(-1, 2 * width)
            total = total + jnp.dot(
                window, bands[r * 3 + d + 1], preferred_element_type=jnp.float32
            )
    return total.astype(jnp.bfloat16).reshape(local, height * halves, 2 * width)


def per_device(frames, clip_ids, norm_gain, space_kernel, time_kernel):
    table = lax.all_gather(clip_ids, "dev", axis=0, tiled=True)
    marks = table + 1
    local = frames.shape[0]
    width = space_kernel.shape[-1]
    devices = lax.axis_size("dev")
    frame_offsets = [
        (kernel_step - TIME_TAPS // 2) * TIME_DILATION for kernel_step in range(TIME_TAPS)
    ]
    current = frames
    for block_index in range(BLOCKS):
        bands = pair_bands(space_kernel[block_index])
        pairs = [
            paired_diagonal(time_kernel[block_index, kernel_step])
            for kernel_step in range(TIME_TAPS)
        ]
        act = normed(current, norm_gain[block_index])
        spat = spatial_convolve(act, bands, width)
        masks = [
            (slide_frames(marks, frame_offset) == marks).astype(jnp.bfloat16)
            for frame_offset in frame_offsets
        ]
        tiled = spat.reshape(local, devices, spat.shape[1] // devices, 2 * width)
        stack = lax.all_to_all(tiled, "dev", split_axis=1, concat_axis=0, tiled=True)
        total = jnp.zeros(
            (stack.shape[0] * stack.shape[1] * stack.shape[2], 2 * width), jnp.float32
        )
        for along_kernel_step in range(TIME_TAPS):
            moved = (
                slide_frames(stack, frame_offsets[along_kernel_step])
                * masks[along_kernel_step][:, None, None, None]
            )
            total = total + jnp.dot(
                moved.reshape(-1, 2 * width),
                pairs[along_kernel_step],
                preferred_element_type=jnp.float32,
            )
        tiles = total.astype(jnp.bfloat16).reshape(stack.shape)
        update = lax.all_to_all(tiles, "dev", split_axis=0, concat_axis=1, tiled=True)
        summed = current.astype(jnp.float32) + update.reshape(current.shape).astype(jnp.float32)
        current = summed.astype(jnp.bfloat16)
    return current


def solution(mesh):
    return jax.shard_map(
        per_device,
        mesh=mesh,
        in_specs=(P(("dp", "dev"), None, None), P(("dp", "dev")), P(), P(), P()),
        out_specs=P(("dp", "dev"), None, None),
        check_vma=False,
    )
```

profile of v0, /device:TPU:0, one launch (start us, length us, event | category | flops | bytes accessed | tf_op | source)
XLA Modules:
  0.0 158.1 jit_solution(12680934166661446889)
XLA Ops:
  0.0 1.3 slice_bitcast_fusion.38
  1.4 1.3 convert_reduce_fusion.1
  2.7 2.1 %reshape.258 = f32[128,32,2]{2,1,0:T(8,128)S(1)} reshape(f32[8192]{0:T(1024)S(1)} %convert_reduce_fusion.1) | data formatting | bytes 65536 | tf_op jit(solution)/shard_map/reshape | solution.py:53
  5.4 0.5 copy-done
  6.2 2.1 %reshape.259 = f32[128,32,2]{2,1,0:T(8,128)S(1)} reshape(f32[8192]{0:T(1024)S(1)} %fusion.16) | data formatting | bytes 65536 | tf_op jit(solution)/shard_map/reshape | solution.py:58
  8.9 0.5 fusion.254
  9.4 0.5 fusion.23
  10.1 3.3 %pad_slice_fusion.8 = (bf16[1,48,64,128]{3,2,1,0:T(8,128)(2,1)S(1)}, bf16[1,48,64,128]{3,2,1,0:T(8,128)(2,1)}, bf16[1,48,64,128]{3,2,1,0:T(8,128)(2,1)}, bf16[1,...) fusion(bf16[1,48,64,128]{3,2,1,0:T(8,128)(2,1)S(1)} %bitcast.172), kind=kLoop, calls=%fused_computation.72 | loop fusion | bytes 7077888 | tf_op jit(solution)/shard_map/slice | solution.py:77
  13.5 1.2 reshape.265
  14.7 0.6 slice_bitcast_fusion.10
  15.9 0.4 convolution_add_fusion.23
  16.3 0.7 copy-done.5
  17.4 0.7 copy-done.4
  18.5 0.8 copy-done.13
  19.3 0.4 convolution_add_fusion.20
  19.7 0.7 copy-done.3
  20.8 0.7 copy-done.2
  21.9 0.8 copy-done.1
  23.1 1.3 fusion
  24.4 6.5 %all-to-all-start = ((bf16[1,8,384,128]{3,2,0,1:T(8,128)(2,1)}), bf16[1,8,384,128]{3,2,0,1:T(8,128)(2,1)S(1)}, u32[]{:S(2)}, u32[]{:S(2)}) async-start(bf16[1,8,384,128]{3,2,0,1:T(8,128)(2,1)} %bitcast.20), calls=%async_computation | async-start | bytes 1572864 | tf_op jit(solution)/shard_map/all_to_all | solution.py:107
  31.6 0.6 dynamic-slice
  32.2 0.7 dynamic-update-slice
  32.9 19.1 %all-reduce.58 = s32[8]{0:T(128)S(1)} all-reduce(s32[8]{0:T(128)S(1)} %dynamic-update-slice), channel_id=1, replica_groups=mesh['dp'=4,'dev'=8] {'dev'}, use_global_device_ids=true, to_apply=%add.58 | all-reduce | flops 8 | bytes 64
  54.7 1.3 fusion.1
  56.0 3.9 %all-to-all-start.1 = ((bf16[8,1,384,128]{3,2,1,0:T(8,128)(2,1)}), bf16[8,1,384,128]{3,2,1,0:T(8,128)(2,1)S(1)}, u32[]{:S(2)}, u32[]{:S(2)}) async-start(bf16[8,1,384,128]{3,2,1,0:T(8,128)(2,1)} %bitcast.38), calls=%async_computation.1 | async-start | bytes 1572864 | tf_op jit(solution)/shard_map/all_to_all | solution.py:122
  60.0 20.6 %all-to-all-done.1 = bf16[8,1,384,128]{3,2,1,0:T(8,128)(2,1)S(1)} async-done(((bf16[8,1,384,128]{3,2,1,0:T(8,128)(2,1)}), bf16[8,1,384,128]{3,2,1,0:T(8,128)(2,1)S(1)}, u32[]{:S(2)}, u32[]{:S(2)}) %all-to-all-start.1) | async-done | bytes 786464 | tf_op jit(solution)/shard_map/all_to_all | solution.py:122
  81.1 3.4 %reshape.276 = f32[128,32,2]{2,1,0:T(8,128)} reshape(f32[8192]{0:T(1024)S(1)} %get-tuple-element.5) | data formatting | bytes 65536 | tf_op jit(solution)/shard_map/reshape | solution.py:53
  84.5 1.9 %reduce_sum.77 = f32[32]{0:T(128)S(1)} reduce(f32[128,32,2]{2,1,0:T(8,128)} %reshape.276, f32[]{:T(128)} %constant.7.clone.1), dimensions={0,2}, to_apply=%region_5.6 | reduce | flops 8160 | bytes 32900 | tf_op jit(solution)/shard_map/reduce_sum | solution.py:53
  87.0 3.4 %reshape.277 = f32[128,32,2]{2,1,0:T(8,128)} reshape(f32[8192]{0:T(1024)S(1)} %fusion.8) | data formatting | bytes 65536 | tf_op jit(solution)/shard_map/reshape | solution.py:58
  90.4 1.9 %reduce_sum.79 = f32[32]{0:T(128)S(1)} reduce(f32[128,32,2]{2,1,0:T(8,128)} %reshape.277, f32[]{:T(128)} %constant.7.clone.1), dimensions={0,2}, to_apply=%region_7.8 | reduce | flops 8160 | bytes 32900 | tf_op jit(solution)/shard_map/reduce_sum | solution.py:59
  92.6 0.5 fusion.253
  93.1 0.5 fusion.15
  93.8 3.3 %pad_slice_fusion = (bf16[1,48,64,128]{3,2,1,0:T(8,128)(2,1)S(1)}, bf16[1,48,64,128]{3,2,1,0:T(8,128)(2,1)}, bf16[1,48,64,128]{3,2,1,0:T(8,128)(2,1)}, bf16[1,48...) fusion(bf16[1,48,64,128]{3,2,1,0:T(8,128)(2,1)S(1)} %bitcast.173), kind=kLoop, calls=%fused_computation.64 | loop fusion | bytes 7077888 | tf_op jit(solution)/shard_map/slice | solution.py:77
  97.1 1.2 reshape.283
  98.7 0.8 copy-done.12
  99.5 0.4 convolution_add_fusion.11
  100.0 0.7 copy-done.11
  101.1 0.7 copy-done.10
  102.1 0.8 copy-done.14
  102.9 0.4 convolution_add_fusion.8
  103.4 0.7 copy-done.9
  104.5 0.7 copy-done.8
  105.5 0.8 copy-done.7
  106.3 0.4 convolution_add_fusion.5
  107.2 23.4 %all_to_all.42 = bf16[1,8,384,128]{3,2,0,1:T(8,128)(2,1)S(1)} all-to-all(bf16[1,8,384,128]{3,2,0,1:T(8,128)(2,1)S(1)} %bitcast.178), channel_id=1, replica_groups=mesh['dp'=4,'dev'=8] {'dev'}, dimensions={1} | all-to-all | bytes 1572864 | tf_op jit(solution)/shard_map/all_to_all | solution.py:107
  131.7 0.4 convolution_add_fusion.3
  133.4 23.4 %all_to_all.43 = bf16[8,1,384,128]{3,2,1,0:T(8,128)(2,1)S(1)} all-to-all(bf16[8,1,384,128]{3,2,1,0:T(8,128)(2,1)S(1)} %bitcast.179), channel_id=1, replica_groups=mesh['dp'=4,'dev'=8] {'dev'}, dimensions={0} | all-to-all | bytes 1572864 | tf_op jit(solution)/shard_map/all_to_all | solution.py:122
  157.1 1.0 fusion.25
  (103 shorter events, 13.3 us)
Async XLA Ops:
  4.8 1.1 copy-start
  10.1 3.3 %copy-start.15 = (bf16[2,3,3,64,64]{4,3,2,1,0:T(8,128)(2,1)S(1)}, bf16[2,3,3,64,64]{4,3,2,1,0:T(8,128)(2,1)}, u32[]{:S(2)}) copy-start(bf16[2,3,3,64,64]{4,3,2,1,0:T(8,128)(2,1)} %param.8) | copy-start | bytes 442372
  14.7 1.1 copy-start.6
  15.9 1.1 copy-start.5
  17.0 1.1 copy-start.4
  18.2 1.1 copy-start.13
  19.3 1.1 copy-start.3
  20.4 1.1 copy-start.2
  21.6 1.1 copy-start.1
  24.4 7.1 %copy-start.20 = (u32[32]{0:T(128)S(1)}, u32[32]{0:T(128)}, u32[]{:S(2)}) copy-start(u32[32]{0:T(128)} %constant.146) | copy-start | bytes 388
  24.4 27.8 %copy-start.16 = (bf16[2,5,64,64]{3,2,1,0:T(8,128)(2,1)S(1)}, bf16[2,5,64,64]{3,2,1,0:T(8,128)(2,1)}, u32[]{:S(2)}) copy-start(bf16[2,5,64,64]{3,2,1,0:T(8,128)(2,1)} %param.9) | copy-start | bytes 245764
  24.4 27.9 %all-to-all-start = ((bf16[1,8,384,128]{3,2,0,1:T(8,128)(2,1)}), bf16[1,8,384,128]{3,2,0,1:T(8,128)(2,1)S(1)}, u32[]{:S(2)}, u32[]{:S(2)}) async-start(bf16[1,8,384,128]{3,2,0,1:T(8,128)(2,1)} %bitcast.20), calls=%async_computation | async-start | bytes 1572864 | tf_op jit(solution)/shard_map/all_to_all | solution.py:107
  56.0 3.9 %copy-start.19 = (f32[64]{0:T(128)S(1)}, f32[64]{0:T(128)}, u32[]{:S(2)}) copy-start(f32[64]{0:T(128)} %get-tuple-element.57) | copy-start | bytes 772
  56.0 24.6 %all-to-all-start.1 = ((bf16[8,1,384,128]{3,2,1,0:T(8,128)(2,1)}), bf16[8,1,384,128]{3,2,1,0:T(8,128)(2,1)S(1)}, u32[]{:S(2)}, u32[]{:S(2)}) async-start(bf16[8,1,384,128]{3,2,1,0:T(8,128)(2,1)} %bitcast.38), calls=%async_computation.1 | async-start | bytes 1572864 | tf_op jit(solution)/shard_map/all_to_all | solution.py:122
  98.4 1.1 copy-start.12
  98.4 1.1 copy-start.18
  99.5 1.1 copy-start.11
  100.7 1.1 copy-start.10
  101.8 1.1 copy-start.14
  101.8 1.1 copy-start.17
  102.9 1.1 copy-start.9
  104.1 1.1 copy-start.8
  105.2 1.1 copy-start.7
where the time goes:
time: 159 us; the launch traced here: 158 us
  blocking collectives  65.8 us (41%)
  local copies, waits for them, and re-layouts  36.7 us (23%)
  waiting for transfers between devices  20.6 us (13%)
  matrix products  12.9 us (8%)
  other arithmetic  10.6 us (7%)
  starting transfers between devices  10.3 us (6%)
    all_to_all x1, blocking collectives, per_device(): lax.all_to_all(tiled, 'dev', split_axis=1, concat_axis=0, tiled=True)  23.4 us
    all_to_all x1, blocking collectives, per_device(): lax.all_to_all(tiles, 'dev', split_axis=0, concat_axis=1, tiled=True)  23.4 us
    all_to_all x1, waiting for transfers between devices, per_device(): lax.all_to_all(tiles, 'dev', split_axis=0, concat_axis=1, tiled=True)  20.6 us
    unnamed x1, blocking collectives  19.1 us
    unnamed x47, local copies, waits for them, and re-layouts  12.1 us
    dot_general x18, matrix products, spatial_convolve(): jnp.dot(window, bands[r * 3 + d + 1], preferred_element_type=jnp.float32)  7.94 us
    slice x2, local copies, waits for them, and re-layouts, spatial_convolve(): padded[:, r:r + height, d + 1:d + 1 + halves, :].reshape(-1, 2 * width)  6.66 us
    all_to_all x1, starting transfers between devices, per_device(): lax.all_to_all(tiled, 'dev', split_axis=1, concat_axis=0, tiled=True)  6.48 us
  transfers between devices with their start and end apart: 2, of which 1 were waited for; matrix products, arithmetic and copies ran while one was open for 1% of the time, Pallas kernels for 0%

commit v1 on v0

v1 whole, which is shorter than its diff:
```python
import functools

import jax
import jax.numpy as jnp
from jax import lax
from jax.experimental import pallas as pl
from jax.experimental.pallas import tpu as pltpu
from jax.sharding import PartitionSpec as P

GROUPS = 32
TIME_TAPS = 5
TIME_DILATION = 2
BLOCKS = 2
LANES = 128
REACH = TIME_TAPS // 2

WHOLE = pl.BlockSpec(memory_space=pltpu.VMEM)
PLACED = pl.BlockSpec(memory_space=pl.ANY)
GRANT = 26 << 20


def lane_tile(index, tiles=1):
    return pl.ds(pl.multiple_of(index * LANES, LANES), tiles * LANES)


def float_tile(frame, index):
    return frame[:, lane_tile(index)].astype(jnp.float32)


def fold_groups(total, width):
    per_group = width // GROUPS
    total = jnp.broadcast_to(jnp.sum(total, axis=0, keepdims=True), total.shape)
    total = total + pltpu.roll(total, width, 1)
    lane = lax.broadcasted_iota(jnp.int32, total.shape, 1)
    step = 1
    while step < per_group:
        ahead, behind = pltpu.roll(total, LANES - step, 1), pltpu.roll(total, step, 1)
        total = total + jnp.where((lane // step) % 2 == 0, ahead, behind)
        step *= 2
    return total[:1]


def by_sublane(values):
    return jnp.sum(values.reshape(-1, 8, LANES), axis=0)


def statistics(frame, tiles, width):
    count = frame.shape[0] * tiles * LANES // GROUPS
    zero = jnp.zeros((8, LANES), jnp.float32)

    def gather(index, total):
        return total + by_sublane(float_tile(frame, index))

    mean = fold_groups(lax.fori_loop(0, tiles, gather, zero, unroll=16), width) / count

    def spread(index, total):
        shifted = float_tile(frame, index) - mean
        return total + by_sublane(shifted * shifted)

    squares = fold_groups(lax.fori_loop(0, tiles, spread, zero, unroll=16), width)
    return mean, lax.rsqrt(squares / count + 1e-06)


def activate(frame, acts, gain, tiles, width):
    mean, scale = statistics(frame, tiles, width)
    scale = scale * jnp.concatenate([gain] * (LANES // width), 1) * 0.5
    height = frame.shape[0]
    lane = lax.broadcasted_iota(jnp.int32, (height, LANES), 1)
    row = lax.broadcasted_iota(jnp.int32, (height, LANES), 0)
    above, level, below = acts

    def put(index, values):
        at = lane_tile(index)
        up, down = pltpu.roll(values, 1, 0), pltpu.roll(values, height - 1, 0)
        above[:, at] = jnp.where(row == 0, 0.0, up).astype(jnp.bfloat16)
        level[:, at] = values.astype(jnp.bfloat16)
        below[:, at] = jnp.where(row == height - 1, 0.0, down).astype(jnp.bfloat16)

    def step(index, last):
        half = (float_tile(frame, index) - mean) * scale
        turned = pltpu.roll(half + half * jnp.tanh(half), width, 1)
        put(index, jnp.where(lane < width, last, turned))
        return turned

    last = lax.fori_loop(0, tiles, step, jnp.zeros((height, LANES), jnp.float32), unroll=8)
    put(tiles, jnp.where(lane < width, last, 0.0))


def spatial(acts, bands, result, tiles):
    height = result.shape[0]
    pack = 32 if tiles % 32 == 0 else 1

    def block(first, carry):
        rows = [
            jnp.concatenate([act[:, lane_tile(first * pack + i, 2)] for act in acts], 1)
            for i in range(pack)
        ]
        total = jnp.dot(jnp.concatenate(rows, 0), bands, preferred_element_type=jnp.float32)
        total = total.astype(jnp.bfloat16)
        for i in range(pack):
            result[:, lane_tile(first * pack + i)] = total[i * height : (i + 1) * height]
        return carry

    lax.fori_loop(0, tiles // pack, block, 0)


def normed_conv(frame, acts, bands, gain, result, tiles, width):
    activate(frame, acts, gain, tiles, width)
    spatial(acts, bands, result, tiles)


def temporal(start, sources, weights, result, tiles):
    height = start.shape[0]
    pack = 32 if tiles % 32 == 0 else 1

    def block(first, carry):
        rows = [
            jnp.concatenate([source[:, lane_tile(first * pack + i)] for source in sources], 1)
            for i in range(pack)
        ]
        total = jnp.dot(jnp.concatenate(rows, 0), weights, preferred_element_type=jnp.float32)
        total = total.astype(jnp.bfloat16).astype(jnp.float32)
        for i in range(pack):
            at = lane_tile(first * pack + i)
            summed = start[:, at].astype(jnp.float32) + total[i * height : (i + 1) * height]
            result[:, at] = summed.astype(jnp.bfloat16)
        return carry

    lax.fori_loop(0, tiles // pack, block, 0)


def marked_weights(table, marks, target, places):
    rows = []
    for mark, place in zip(marks, places):
        same = (mark == target).astype(jnp.float32)
        rows.append((table[place].astype(jnp.float32) * same).astype(jnp.bfloat16))
    return jnp.concatenate(rows, 0)


def mark_of(frame, tiles):
    return frame[0:16, lane_tile(tiles)].astype(jnp.float32)[:1]


def fetch(source, target, sem):
    copy = pltpu.make_async_copy(source, target, sem)
    copy.start()
    copy.wait()


def mark_kernel(ids, frame, marked, sem):
    columns = frame.shape[-1]
    copy = pltpu.make_async_copy(frame.at[0], marked.at[:, pl.ds(0, columns)], sem)
    copy.start()
    marked[:, columns:] = jnp.full((marked.shape[0], LANES), ids[0].astype(jnp.float32)).astype(
        jnp.bfloat16
    )
    copy.wait()


def mark_frames(frames, clip_ids):
    _, height, columns = frames.shape
    return pl.pallas_call(
        mark_kernel,
        out_shape=jax.ShapeDtypeStruct((height, columns + LANES), frames.dtype),
        in_specs=[pl.BlockSpec(memory_space=pltpu.SMEM), PLACED],
        out_specs=WHOLE,
        scratch_shapes=[pltpu.SemaphoreType.DMA],
        compiler_params=pltpu.CompilerParams(vmem_limit_bytes=4 << 20),
        name="mark_frames",
    )(clip_ids, frames)


def build_bands(space, bands):
    width = space.shape[-1]
    blank = jnp.zeros((width, width), jnp.bfloat16)
    for block in range(BLOCKS):
        for r in range(3):
            for a in range(4):
                pair = [space[block, r, a - b] if 0 <= a - b <= 2 else blank for b in (0, 1)]
                bands[block, pl.ds((r * 4 + a) * width, width), :] = jnp.concatenate(pair, 1)


def build_table(time, table, near):
    width = time.shape[-1]
    blank = jnp.zeros((width, width), jnp.bfloat16)
    for block in range(BLOCKS):
        for entry in range(TIME_TAPS + 2):
            if 1 <= entry <= TIME_TAPS:
                tap = jnp.where(near, entry - 1, TIME_TAPS - entry)
                matrix = time[block, tap]
            else:
                matrix = blank
            upper = jnp.concatenate([matrix, blank], 1)
            lower = jnp.concatenate([blank, matrix], 1)
            table[block, entry] = jnp.concatenate([upper, lower], 0)


def acts_scratch(height, columns):
    return [pltpu.VMEM((height, columns + LANES), jnp.bfloat16)] * 3


def like(frame, lanes=0):
    return jax.ShapeDtypeStruct((frame.shape[0], frame.shape[1] + lanes), jnp.bfloat16)


def estimate(frames):
    return pl.CostEstimate(
        flops=frames * 1_000_000_000, bytes_accessed=frames * 4_000_000, transcendentals=0
    )


def own_kernel(dims, where, frame, gains, space, time, conv, bands, table, *acts):
    tiles, width = dims
    build_bands(space, bands)
    build_table(time, table, where[0] == 1)
    normed_conv(frame, acts, bands[0], gains[0:1], conv, tiles, width)
    conv[:, lane_tile(tiles)] = frame[:, lane_tile(tiles)]


def own_call(where, frame, gains, space, time):
    height, columns = frame.shape
    width = space.shape[-1]
    tiles = columns // LANES - 1
    return pl.pallas_call(
        functools.partial(own_kernel, (tiles, width)),
        out_shape=(
            like(frame),
            jax.ShapeDtypeStruct((BLOCKS, 12 * width, LANES), jnp.bfloat16),
            jax.ShapeDtypeStruct((BLOCKS, TIME_TAPS + 2, LANES, LANES), jnp.bfloat16),
        ),
        in_specs=[pl.BlockSpec(memory_space=pltpu.SMEM)] + [WHOLE] * 4,
        out_specs=(WHOLE,) * 3,
        scratch_shapes=acts_scratch(height, columns),
        compiler_params=pltpu.CompilerParams(vmem_limit_bytes=GRANT),
        cost_estimate=estimate(1),
        name="own",
    )(where, frame, gains, space, time)


def next_kernel(dims, where, left, right, gains, bands, xn, sn, xo, so, *rest):
    tiles, width = dims
    acts, sem = rest[:3], rest[3]
    near, middle = where[0] == 1, where[1] == 1

    def conv(result, frame):
        normed_conv(frame, acts, bands[0], gains[0:1], result, tiles, width)
        result[:, lane_tile(tiles)] = frame[:, lane_tile(tiles)]

    pl.when(near)(lambda: fetch(right, xn, sem))
    pl.when(jnp.logical_not(near))(lambda: fetch(left, xn, sem))
    conv(sn, xn)

    @pl.when(jnp.logical_not(middle))
    def _():
        so[...] = jnp.zeros(so.shape, so.dtype)

    @pl.when(middle)
    def _():
        pl.when(near)(lambda: fetch(left, xo, sem))
        pl.when(jnp.logical_not(near))(lambda: fetch(right, xo, sem))
        conv(so, xo)


def next_call(where, left, right, gains, bands):
    height, columns = left.shape
    tiles, width = columns // LANES - 1, gains.shape[-1]
    return pl.pallas_call(
        functools.partial(next_kernel, (tiles, width)),
        out_shape=(like(left),) * 4,
        in_specs=[pl.BlockSpec(memory_space=pltpu.SMEM), PLACED, PLACED, WHOLE, WHOLE],
        out_specs=(WHOLE,) * 4,
        scratch_shapes=acts_scratch(height, columns) + [pltpu.SemaphoreType.DMA],
        compiler_params=pltpu.CompilerParams(vmem_limit_bytes=GRANT),
        cost_estimate=estimate(2),
        name="next",
    )(where, left, right, gains, bands)


def places(middle, target):
    one = middle.astype(jnp.int32)
    lie = [one, one + 1, one + 2, 3 - 3 * one]
    return [at - lie[target] + REACH + 1 for at in lie]


def clamped(entries):
    return [jnp.clip(entry, 0, TIME_TAPS + 1) for entry in entries]


def after_kernel(dims, *refs):
    tiles, width = dims
    where, ends, plus, minus, gains, bands, table, xs, ss, sn, so = refs[:11]
    xa, sa, xs1, ss1 = refs[11:15]
    acts, sem = refs[15:18], refs[18]
    near, middle = where[0] == 1, where[1] == 1
    outer = jnp.logical_not(middle)

    pl.when(middle)(lambda: fetch(ends, xa, sem))
    pl.when(outer & near)(lambda: fetch(minus, xa, sem))
    pl.when(outer & jnp.logical_not(near))(lambda: fetch(plus, xa, sem))
    normed_conv(xa, acts, bands[0], gains[0:1], sa, tiles, width)
    sa[:, lane_tile(tiles)] = xa[:, lane_tile(tiles)]

    sources = (ss, sn, sa, so)
    marks = [mark_of(source, tiles) for source in sources]
    weights = marked_weights(table.at[0], marks, marks[0], clamped(places(middle, 0)))
    temporal(xs, sources, weights, xs1, tiles)
    normed_conv(xs1, acts, bands[1], gains[1:2], ss1, tiles, width)


def after_call(where, ends, plus, minus, gains, bands, table, xs, ss, sn, so):
    height, columns = xs.shape
    tiles, width = columns // LANES - 1, gains.shape[-1]
    return pl.pallas_call(
        functools.partial(after_kernel, (tiles, width)),
        out_shape=(like(xs), like(xs), like(xs, -LANES), like(xs, -LANES)),
        in_specs=[pl.BlockSpec(memory_space=pltpu.SMEM)] + [PLACED] * 3 + [WHOLE] * 7,
        out_specs=(WHOLE,) * 4,
        scratch_shapes=acts_scratch(height, columns) + [pltpu.SemaphoreType.DMA],
        compiler_params=pltpu.CompilerParams(vmem_limit_bytes=GRANT),
        cost_estimate=estimate(2),
        name="after",
    )(where, ends, plus, minus, gains, bands, table, xs, ss, sn, so)


def last_kernel(dims, *refs):
    tiles, width = dims
    where, corner, gains, bands, table, ss, sn, so_mid, sa, xn, xo, xa, xs1, ss1 = refs[:14]
    out = refs[14]
    acts = refs[15:18]
    so, x1, sn1, sa1, so1, sem = refs[18:]
    middle = where[1] == 1
    outer = jnp.logical_not(middle)

    pl.when(middle)(lambda: fetch(so_mid, so, sem))
    pl.when(outer)(lambda: fetch(corner, so, sem))
    sources = (ss, sn, sa, so)
    marks = [mark_of(source, tiles) for source in sources]

    def both(target, start, result):
        entries = clamped(places(middle, target))
        weights = marked_weights(table.at[0], marks, marks[target], entries)
        temporal(start, sources, weights, x1, tiles)
        normed_conv(x1, acts, bands[1], gains[1:2], result, tiles, width)

    both(1, xn, sn1)
    both(2, xa, sa1)

    @pl.when(outer)
    def _():
        so1[...] = jnp.zeros(so1.shape, so1.dtype)

    pl.when(middle)(lambda: both(3, xo, so1))
    weights = marked_weights(table.at[1], marks, marks[0], clamped(places(middle, 0)))
    temporal(xs1, (ss1, sn1, sa1, so1), weights, out.at[0], tiles)


def last_call(where, corner, gains, bands, table, ss, sn, so, sa, xn, xo, xa, xs1, ss1):
    height, columns = xn.shape
    tiles, width = columns // LANES - 1, gains.shape[-1]
    plain = pltpu.VMEM((height, columns - LANES), jnp.bfloat16)
    return pl.pallas_call(
        functools.partial(last_kernel, (tiles, width)),
        out_shape=jax.ShapeDtypeStruct((1, height, columns - LANES), jnp.bfloat16),
        in_specs=[pl.BlockSpec(memory_space=pltpu.SMEM), PLACED] + [WHOLE] * 12,
        out_specs=WHOLE,
        scratch_shapes=acts_scratch(height, columns)
        + [pltpu.VMEM((height, columns), jnp.bfloat16)]
        + [plain] * 4
        + [pltpu.SemaphoreType.DMA],
        compiler_params=pltpu.CompilerParams(vmem_limit_bytes=GRANT),
        cost_estimate=estimate(3),
        name="last",
    )(where, corner, gains, bands, table, ss, sn, so, sa, xn, xo, xa, xs1, ss1)


def moved(values, hops):
    pairs = [(TIME_DILATION * a + c, TIME_DILATION * b + c) for a, b in hops for c in (0, 1)]
    return lax.ppermute(values, "dev", pairs)


def on_a_line(frames, clip_ids, norm_gain, space_kernel, time_kernel):
    chip = lax.axis_index("dev") // TIME_DILATION
    near, middle = chip < 2, (chip == 1) | (chip == 2)
    where = jnp.stack([near, middle]).astype(jnp.int32)
    xs = mark_frames(frames, clip_ids)
    left = moved(xs, [(0, 1), (1, 2), (2, 3)])
    right = moved(xs, [(1, 0), (2, 1), (3, 2)])
    ends = moved(xs, [(0, 2), (3, 1)])
    ss, bands, table = own_call(where, xs, norm_gain, space_kernel, time_kernel)
    corner = moved(ss, [(0, 3), (3, 0)])
    left, _ = lax.optimization_barrier((left, ss))
    right, _ = lax.optimization_barrier((right, ss))
    plus = moved(left, [(2, 3)])
    minus = moved(right, [(1, 0)])
    xn, sn, xo, so = next_call(where, left, right, norm_gain, bands)
    xa, sa, xs1, ss1 = after_call(
        where, ends, plus, minus, norm_gain, bands, table, xs, ss, sn, so
    )
    return last_call(
        where, corner, norm_gain, bands, table, ss, sn, so, sa, xn, xo, xa, xs1, ss1
    )


def conv_kernel(dims, block, frame, gains, bands, conv, *acts):
    tiles, width = dims
    normed_conv(frame, acts, bands[block], gains[block : block + 1], conv, tiles, width)
    conv[:, lane_tile(tiles)] = frame[:, lane_tile(tiles)]


def conv_call(block, frame, gains, bands):
    height, columns = frame.shape
    tiles, width = columns // LANES - 1, gains.shape[-1]
    return pl.pallas_call(
        functools.partial(conv_kernel, (tiles, width), block),
        out_shape=like(frame),
        in_specs=[WHOLE] * 3,
        out_specs=WHOLE,
        scratch_shapes=acts_scratch(height, columns),
        compiler_params=pltpu.CompilerParams(vmem_limit_bytes=GRANT),
        name="conv",
    )(frame, gains, bands)


def mix_kernel(tiles, block, frame, table, *refs):
    sources, result = refs[:TIME_TAPS], refs[TIME_TAPS]
    marks = [mark_of(source, tiles) for source in sources]
    entries = range(1, TIME_TAPS + 1)
    weights = marked_weights(table.at[block], marks, marks[REACH], entries)
    temporal(frame, sources, weights, result, tiles)
    result[:, lane_tile(tiles)] = frame[:, lane_tile(tiles)]


def mix_call(block, frame, table, sources):
    return pl.pallas_call(
        functools.partial(mix_kernel, frame.shape[1] // LANES - 1, block),
        out_shape=like(frame),
        in_specs=[WHOLE] * (2 + TIME_TAPS),
        out_specs=WHOLE,
        compiler_params=pltpu.CompilerParams(vmem_limit_bytes=GRANT),
        name="mix",
    )(frame, table, *sources)


def by_relays(frames, clip_ids, norm_gain, space_kernel, time_kernel):
    chips = lax.axis_size("dev") // TIME_DILATION
    up = [(i, i + 1) for i in range(chips - 1)]
    down = [(i + 1, i) for i in range(chips - 1)]
    frame = mark_frames(frames, clip_ids)
    where = jnp.ones((2,), jnp.int32)
    conv, bands, table = own_call(where, frame, norm_gain, space_kernel, time_kernel)
    for block in range(BLOCKS):
        if block > 0:
            conv = conv_call(block, frame, norm_gain, bands)
        sources = [conv]
        for _ in range(REACH):
            sources = [moved(sources[0], up)] + sources + [moved(sources[-1], down)]
        frame = mix_call(block, frame, table, sources)
    return frame[None, :, : frames.shape[2]]


def per_device(*args):
    return (on_a_line if lax.axis_size("dev") == 8 else by_relays)(*args)


def solution(mesh):
    return jax.shard_map(
        per_device,
        mesh=mesh,
        in_specs=(P(("dp", "dev"), None, None), P(("dp", "dev")), P(), P(), P()),
        out_specs=P(("dp", "dev"), None, None),
        check_vma=False,
    )
```

time: 159 us -> 94.6 us (0.59)
  the two profiles are of different devices: /device:TPU:0 before, /device:TPU:16 now
where the time goes in v1:
time: 94.6 us; the launch traced here: 94.3 us
  waiting for transfers between devices  43.2 us (46%)
  Pallas kernels  37.7 us (40%)
  starting transfers between devices  9.89 us (10%)
  local copies, waits for them, and re-layouts  2.64 us (3%)
    ppermute x6, waiting for transfers between devices, moved(): return lax.ppermute(values, 'dev', pairs)  43.2 us
    pallas_call x1, Pallas kernels, last_call(): pl.pallas_call(functools.partial(last_kernel, (tiles, width)), out_shape=...  17 us
    ppermute x6, starting transfers between devices, moved(): return lax.ppermute(values, 'dev', pairs)  9.89 us
    pallas_call x1, Pallas kernels, after_call(): pl.pallas_call(functools.partial(after_kernel, (tiles, width)), out_shape...  8.81 us
    pallas_call x1, Pallas kernels, next_call(): pl.pallas_call(functools.partial(next_kernel, (tiles, width)), out_shape=...  7.61 us
    pallas_call x1, Pallas kernels, own_call(): pl.pallas_call(functools.partial(own_kernel, (tiles, width)), out_shape=(...  4.19 us
    unnamed x8, local copies, waits for them, and re-layouts  2.64 us
  transfers between devices with their start and end apart: 6, of which 2 were waited for; matrix products, arithmetic and copies ran while one was open for 0% of the time, Pallas kernels for 22%

profile of v1, /device:TPU:16, one launch (start us, length us, event | category | flops | bytes accessed | tf_op | source)
XLA Modules:
  0.0 94.3 jit_solution(8225809094152739785)
XLA Ops:
  0.7 0.0 copy-start
  0.7 1.1 %copy-done = bf16[1,48,8192]{2,1,0:T(8,128)(2,1)S(1)} copy-done((bf16[1,48,8192]{2,1,0:T(8,128)(2,1)S(1)}, bf16[1,48,8192]{2,1,0:T(8,128)(2,1)}, u32[]{:S(2)}) %copy-start) | copy-done | bytes 786456
  1.8 0.0 copy-start.1
  1.8 0.1 mark_frames.1.frame.refs_7_
  1.9 3.5 %collective-permute-start.1 = (bf16[48,8320]{1,0:T(8,128)(2,1)S(1)}, bf16[48,8320]{1,0:T(8,128)(2,1)S(1)}, u32[]{:S(2)}, u32[]{:S(2)}) collective-permute-start(bf16[48,8320]{1,0:T(8,128)(2,1)S(1)} %mark_frames.1.frame.refs_7_), channel_id=1, source_target_pairs={{0,2},{1,3},{2,4},{3,5},{4,6},{5,7},{8,10},{9,11},{10,12},{11,13},... | collective-permute-start | bytes 2396168 | tf_op jit(solution)/shard_map/ppermute | solution.py:378
  5.4 2.4 %collective-permute-start.2 = (bf16[48,8320]{1,0:T(8,128)(2,1)S(1)}, bf16[48,8320]{1,0:T(8,128)(2,1)S(1)}, u32[]{:S(2)}, u32[]{:S(2)}) collective-permute-start(bf16[48,8320]{1,0:T(8,128)(2,1)S(1)} %mark_frames.1.frame.refs_7_), channel_id=1, source_target_pairs={{2,0},{3,1},{4,2},{5,3},{6,4},{7,5},{10,8},{11,9},{12,10},{13,11},... | collective-permute-start | bytes 2396168 | tf_op jit(solution)/shard_map/ppermute | solution.py:378
  7.7 1.3 %collective-permute-start.3 = (bf16[48,8320]{1,0:T(8,128)(2,1)S(1)}, bf16[48,8320]{1,0:T(8,128)(2,1)S(1)}, u32[]{:S(2)}, u32[]{:S(2)}) collective-permute-start(bf16[48,8320]{1,0:T(8,128)(2,1)S(1)} %mark_frames.1.frame.refs_7_), channel_id=1, source_target_pairs={{0,4},{1,5},{6,2},{7,3},{8,12},{9,13},{14,10},{15,11},{16,20},{17,... | collective-permute-start | bytes 2396168 | tf_op jit(solution)/shard_map/ppermute | solution.py:378
  9.1 0.0 copy-start.3
  9.1 0.1 add_convert_fusion.where.refs_0_
  9.2 0.0 copy-done.1
  9.2 0.6 copy-done.3
  9.8 0.0 copy-start.2
  9.8 0.9 copy-done.2
  10.7 4.2 %own.1 = (bf16[48,8320]{1,0:T(8,128)(2,1)S(1)}, bf16[2,768,128]{2,1,0:T(8,128)(2,1)S(1)}, bf16[2,7,128,128]{3,2,1,0:T(8,128)(2,1)S(1)}) custom-call(s32[2]{0:T(128)S(1)} %add_convert_fusion.where.refs_0_, bf16[48,8320]{1,0:T(8,128)(2,1)S(1)} %mark_frames.1.frame.refs_7_, f32[2,64]{1,0:T(2,128)S(1)} %copy-done.3, bf16[2,3,3,64,64]{4,3,2,1,0:T(8,128)(2,1)S(1)} %copy-done.1, ...), custom_call_target="tpu_custom_call" | custom-call | flops 1000000000 | bytes 4000000 | tf_op jit(solution)/shard_map/own/pallas_call | solution.py:224
  14.9 42.7 %collective-permute-done.1.left = bf16[48,8320]{1,0:T(8,128)(2,1)S(1)} collective-permute-done((bf16[48,8320]{1,0:T(8,128)(2,1)S(1)}, bf16[48,8320]{1,0:T(8,128)(2,1)S(1)}, u32[]{:S(2)}, u32[]{:S(2)}) %collective-permute-start.1) | collective-permute-done | bytes 798752 | tf_op jit(solution)/shard_map/ppermute | solution.py:378
  57.6 0.0 collective-permute-done.2.right
  57.6 1.3 %collective-permute-start.4 = (bf16[48,8320]{1,0:T(8,128)(2,1)S(1)}, bf16[48,8320]{1,0:T(8,128)(2,1)S(1)}, u32[]{:S(2)}, u32[]{:S(2)}) collective-permute-start(bf16[48,8320]{1,0:T(8,128)(2,1)S(1)} %collective-permute-done.1.left), channel_id=1, source_target_pairs={{4,6},{5,7},{12,14},{13,15},{20,22},{21,23},{28,30},{29,31}} | collective-permute-start | bytes 2396168 | tf_op jit(solution)/shard_map/ppermute | solution.py:378
  58.9 0.7 collective-permute-start.5
  59.6 0.7 collective-permute-start
  60.3 7.6 %next.1 = (bf16[48,8320]{1,0:T(8,128)(2,1)S(1)}, bf16[48,8320]{1,0:T(8,128)(2,1)S(1)}, bf16[48,8320]{1,0:T(8,128)(2,1)S(1)}, bf16[48,8320]{1,0:T(8,128)(2,1)S(1)}) custom-call(s32[2]{0:T(128)S(1)} %add_convert_fusion.where.refs_0_, bf16[48,8320]{1,0:T(8,128)(2,1)S(1)} %collective-permute-done.1.left, bf16[48,8320]{1,0:T(8,128)(2,1)S(1)} %collective-permute-done.2.right, ...), custom_call_target="tpu_custom_call" | custom-call | flops 2000000000 | bytes 8000000 | tf_op jit(solution)/shard_map/next/pallas_call | solution.py:267
  68.0 0.0 collective-permute-done.3.refs_1_
  68.0 0.5 collective-permute-done.4.refs_2_
  68.5 0.0 collective-permute-done.5.refs_3_
  68.5 8.8 %after.1 = (bf16[48,8320]{1,0:T(8,128)(2,1)S(1)}, bf16[48,8320]{1,0:T(8,128)(2,1)S(1)}, bf16[48,8192]{1,0:T(8,128)(2,1)S(1)}, bf16[48,8192]{1,0:T(8,128)(2,1)S(1)}) custom-call(s32[2]{0:T(128)S(1)} %add_convert_fusion.where.refs_0_, bf16[48,8320]{1,0:T(8,128)(2,1)S(1)} %collective-permute-done.3.refs_1_, ...), custom_call_target="tpu_custom_call" | custom-call | flops 2000000000 | bytes 8000000 | tf_op jit(solution)/shard_map/after/pallas_call | solution.py:313
  77.3 0.0 collective-permute-done.refs_1_
  77.3 17.0 %last.1 = bf16[1,48,8192]{2,1,0:T(8,128)(2,1)} custom-call(s32[2]{0:T(128)S(1)} %add_convert_fusion.where.refs_0_, bf16[48,8320]{1,0:T(8,128)(2,1)S(1)} %collective-permute-done.refs_1_, f32[2,64]{1,0:T(2,128)S(1)} %copy-done.3, bf16[2,768,128]{2,1,0:T(8,128)(2,1)S(1)} %get-tuple-element.19.bands.refs_5_.refs_3_, ...), custom_call_target="tpu_custom_call" | custom-call | flops 3000000000 | bytes 12000000 | tf_op jit(solution)/shard_map/last/pallas_call | solution.py:361
Async XLA Ops:
  0.7 1.1 %copy-start = (bf16[1,48,8192]{2,1,0:T(8,128)(2,1)S(1)}, bf16[1,48,8192]{2,1,0:T(8,128)(2,1)}, u32[]{:S(2)}) copy-start(bf16[1,48,8192]{2,1,0:T(8,128)(2,1)} %frame.1) | copy-start | bytes 2359300
  1.8 7.4 %copy-start.1 = (bf16[2,3,3,64,64]{4,3,2,1,0:T(8,128)(2,1)S(1)}, bf16[2,3,3,64,64]{4,3,2,1,0:T(8,128)(2,1)}, u32[]{:S(2)}) copy-start(bf16[2,3,3,64,64]{4,3,2,1,0:T(8,128)(2,1)} %space.1) | copy-start | bytes 442372
  1.9 55.7 %collective-permute-start.1 = (bf16[48,8320]{1,0:T(8,128)(2,1)S(1)}, bf16[48,8320]{1,0:T(8,128)(2,1)S(1)}, u32[]{:S(2)}, u32[]{:S(2)}) collective-permute-start(bf16[48,8320]{1,0:T(8,128)(2,1)S(1)} %mark_frames.1.frame.refs_7_), channel_id=1, source_target_pairs={{0,2},{1,3},{2,4},{3,5},{4,6},{5,7},{8,10},{9,11},{10,12},{11,13},... | collective-permute-start | bytes 2396168 | tf_op jit(solution)/shard_map/ppermute | solution.py:378
  5.4 52.2 %collective-permute-start.2 = (bf16[48,8320]{1,0:T(8,128)(2,1)S(1)}, bf16[48,8320]{1,0:T(8,128)(2,1)S(1)}, u32[]{:S(2)}, u32[]{:S(2)}) collective-permute-start(bf16[48,8320]{1,0:T(8,128)(2,1)S(1)} %mark_frames.1.frame.refs_7_), channel_id=1, source_target_pairs={{2,0},{3,1},{4,2},{5,3},{6,4},{7,5},{10,8},{11,9},{12,10},{13,11},... | collective-permute-start | bytes 2396168 | tf_op jit(solution)/shard_map/ppermute | solution.py:378
  7.7 60.2 %collective-permute-start.3 = (bf16[48,8320]{1,0:T(8,128)(2,1)S(1)}, bf16[48,8320]{1,0:T(8,128)(2,1)S(1)}, u32[]{:S(2)}, u32[]{:S(2)}) collective-permute-start(bf16[48,8320]{1,0:T(8,128)(2,1)S(1)} %mark_frames.1.frame.refs_7_), channel_id=1, source_target_pairs={{0,4},{1,5},{6,2},{7,3},{8,12},{9,13},{14,10},{15,11},{16,20},{17,... | collective-permute-start | bytes 2396168 | tf_op jit(solution)/shard_map/ppermute | solution.py:378
  9.1 0.7 copy-start.3
  9.8 0.9 copy-start.2
  57.6 10.9 %collective-permute-start.4 = (bf16[48,8320]{1,0:T(8,128)(2,1)S(1)}, bf16[48,8320]{1,0:T(8,128)(2,1)S(1)}, u32[]{:S(2)}, u32[]{:S(2)}) collective-permute-start(bf16[48,8320]{1,0:T(8,128)(2,1)S(1)} %collective-permute-done.1.left), channel_id=1, source_target_pairs={{4,6},{5,7},{12,14},{13,15},{20,22},{21,23},{28,30},{29,31}} | collective-permute-start | bytes 2396168 | tf_op jit(solution)/shard_map/ppermute | solution.py:378
  58.9 9.6 %collective-permute-start.5 = (bf16[48,8320]{1,0:T(8,128)(2,1)S(1)}, bf16[48,8320]{1,0:T(8,128)(2,1)S(1)}, u32[]{:S(2)}, u32[]{:S(2)}) collective-permute-start(bf16[48,8320]{1,0:T(8,128)(2,1)S(1)} %collective-permute-done.2.right), channel_id=1, source_target_pairs={{2,0},{3,1},{10,8},{11,9},{18,16},{19,17},{26,24},{27,25}} | collective-permute-start | bytes 2396168 | tf_op jit(solution)/shard_map/ppermute | solution.py:378
  59.6 17.7 %collective-permute-start = (bf16[48,8320]{1,0:T(8,128)(2,1)S(1)}, bf16[48,8320]{1,0:T(8,128)(2,1)S(1)}, u32[]{:S(2)}, u32[]{:S(2)}) collective-permute-start(bf16[48,8320]{1,0:T(8,128)(2,1)S(1)} %get-tuple-element.18.refs_8_.refs_5_), channel_id=1, source_target_pairs={{0,6},{1,7},{6,0},{7,1},{8,14},{9,15},{14,8},{15,9},{16,22},{17,23... | collective-permute-start | bytes 2396168 | tf_op jit(solution)/shard_map/ppermute | solution.py:378

commit v2 on v1

v2 whole, which is shorter than its diff:
```python
import functools

import jax
import jax.numpy as jnp
from jax import lax
from jax.experimental import pallas as pl
from jax.experimental.pallas import tpu as pltpu
from jax.sharding import PartitionSpec as P

GROUPS = 32
TIME_TAPS = 5
TIME_DILATION = 2
BLOCKS = 2
LANES = 128
REACH = TIME_TAPS // 2

WHOLE = pl.BlockSpec(memory_space=pltpu.VMEM)
PLACED = pl.BlockSpec(memory_space=pl.ANY)
GRANT = 26 << 20


def lane_tile(index, tiles=1):
    return pl.ds(pl.multiple_of(index * LANES, LANES), tiles * LANES)


def float_tile(frame, index):
    return frame[:, lane_tile(index)].astype(jnp.float32)


def fold_groups(total, width):
    per_group = width // GROUPS
    total = jnp.broadcast_to(jnp.sum(total, axis=0, keepdims=True), total.shape)
    total = total + pltpu.roll(total, width, 1)
    lane = lax.broadcasted_iota(jnp.int32, total.shape, 1)
    step = 1
    while step < per_group:
        ahead, behind = pltpu.roll(total, LANES - step, 1), pltpu.roll(total, step, 1)
        total = total + jnp.where((lane // step) % 2 == 0, ahead, behind)
        step *= 2
    return total[:1]


def by_sublane(values):
    return jnp.sum(values.reshape(-1, 8, LANES), axis=0)


def statistics(frame, tiles, width):
    share = frame.shape[0] * LANES // GROUPS
    pivot = fold_groups(by_sublane(float_tile(frame, 0)), width) / share
    zero = jnp.zeros((8, LANES), jnp.float32)

    def gather(index, totals):
        shifted = float_tile(frame, index) - pivot
        return totals[0] + by_sublane(shifted), totals[1] + by_sublane(shifted * shifted)

    sums, squares = lax.fori_loop(0, tiles, gather, (zero, zero), unroll=16)
    offset = fold_groups(sums, width) / (share * tiles)
    spread = fold_groups(squares, width) / (share * tiles) - offset * offset
    return pivot + offset, lax.rsqrt(jnp.maximum(spread, 0.0) + 1e-06)


def activate(frame, act, gain, tiles, width):
    mean, scale = statistics(frame, tiles, width)
    scale = scale * jnp.concatenate([gain] * (LANES // width), 1) * 0.5
    height = frame.shape[0]
    lane = lax.broadcasted_iota(jnp.int32, (height, LANES), 1)

    def step(index, last):
        half = (float_tile(frame, index) - mean) * scale
        turned = pltpu.roll(half + half * jnp.tanh(half), width, 1)
        act[:, lane_tile(index)] = jnp.where(lane < width, last, turned).astype(jnp.bfloat16)
        return turned

    last = lax.fori_loop(0, tiles, step, jnp.zeros((height, LANES), jnp.float32), unroll=16)
    act[:, lane_tile(tiles)] = jnp.where(lane < width, last, 0.0).astype(jnp.bfloat16)


def packed(tiles):
    return 32 if tiles % 32 == 0 else 1


def spatial(act, bands, result, tiles):
    height = result.shape[0]
    pack = packed(tiles)
    row = lax.broadcasted_iota(jnp.int32, (height, LANES), 0)

    def block(first, carry):
        rows = [act[:, lane_tile(first * pack + i, 2)] for i in range(pack)]
        total = jnp.dot(jnp.concatenate(rows, 0), bands, preferred_element_type=jnp.float32)
        for i in range(pack):
            part = total[i * height : (i + 1) * height]
            above = jnp.where(row == 0, 0.0, pltpu.roll(part[:, :LANES], 1, 0))
            below = pltpu.roll(part[:, 2 * LANES :], height - 1, 0)
            below = jnp.where(row == height - 1, 0.0, below)
            summed = above + part[:, LANES : 2 * LANES] + below
            result[:, lane_tile(first * pack + i)] = summed.astype(jnp.bfloat16)
        return carry

    lax.fori_loop(0, tiles // pack, block, 0)


def normed_conv(frame, act, bands, gain, result, tiles, width):
    activate(frame, act, gain, tiles, width)
    spatial(act, bands, result, tiles)


def temporal(sources, weights, tiles, emit):
    height = sources[0].shape[0]
    pack = packed(tiles)

    def block(first, carry):
        rows = [
            jnp.concatenate([source[:, lane_tile(first * pack + i)] for source in sources], 1)
            for i in range(pack)
        ]
        total = jnp.dot(jnp.concatenate(rows, 0), weights, preferred_element_type=jnp.float32)
        for i in range(pack):
            part = total[i * height : (i + 1) * height]
            for target in range(weights.shape[1] // LANES):
                sums = part[:, target * LANES : (target + 1) * LANES]
                emit(lane_tile(first * pack + i), target, sums)
        return carry

    lax.fori_loop(0, tiles // pack, block, 0)


def adding(starts, results):
    def emit(at, target, sums):
        update = sums.astype(jnp.bfloat16).astype(jnp.float32)
        summed = starts[target][:, at].astype(jnp.float32) + update
        results[target][:, at] = summed.astype(jnp.bfloat16)

    return emit


def marked_weights(table, marks, target, places):
    rows = []
    for mark, place in zip(marks, places):
        same = (mark == target).astype(jnp.float32)
        rows.append((table[place].astype(jnp.float32) * same).astype(jnp.bfloat16))
    return jnp.concatenate(rows, 0)


def mark_of(frame, tiles):
    return frame[0:16, lane_tile(tiles)].astype(jnp.float32)[:1]


def fetch(source, target, sem):
    copy = pltpu.make_async_copy(source, target, sem)
    copy.start()
    copy.wait()


def mark_kernel(ids, frame, marked, sem):
    columns = frame.shape[-1]
    copy = pltpu.make_async_copy(frame.at[0], marked.at[:, pl.ds(0, columns)], sem)
    copy.start()
    marked[:, columns:] = jnp.full((marked.shape[0], LANES), ids[0].astype(jnp.float32)).astype(
        jnp.bfloat16
    )
    copy.wait()


def mark_frames(frames, clip_ids):
    _, height, columns = frames.shape
    return pl.pallas_call(
        mark_kernel,
        out_shape=jax.ShapeDtypeStruct((height, columns + LANES), frames.dtype),
        in_specs=[pl.BlockSpec(memory_space=pltpu.SMEM), PLACED],
        out_specs=WHOLE,
        scratch_shapes=[pltpu.SemaphoreType.DMA],
        compiler_params=pltpu.CompilerParams(vmem_limit_bytes=4 << 20),
        name="mark_frames",
    )(clip_ids, frames)


def build_bands(space, bands):
    width = space.shape[-1]
    blank = jnp.zeros((width, width), jnp.bfloat16)
    for block in range(BLOCKS):
        for r in range(3):
            for a in range(4):
                pair = [space[block, r, a - b] if 0 <= a - b <= 2 else blank for b in (0, 1)]
                at = pl.ds(a * width, width), pl.ds(r * LANES, LANES)
                bands[(block, *at)] = jnp.concatenate(pair, 1)


def build_table(time, table, near):
    width = time.shape[-1]
    blank = jnp.zeros((width, width), jnp.bfloat16)
    for block in range(BLOCKS):
        for entry in range(TIME_TAPS + 2):
            if 1 <= entry <= TIME_TAPS:
                tap = jnp.where(near, entry - 1, TIME_TAPS - entry)
                matrix = time[block, tap]
            else:
                matrix = blank
            upper = jnp.concatenate([matrix, blank], 1)
            lower = jnp.concatenate([blank, matrix], 1)
            table[block, entry] = jnp.concatenate([upper, lower], 0)


def act_scratch(height, columns):
    return [pltpu.VMEM((height, columns), jnp.bfloat16)]


def like(frame, lanes=0):
    return jax.ShapeDtypeStruct((frame.shape[0], frame.shape[1] + lanes), jnp.bfloat16)


def estimate(frames):
    return pl.CostEstimate(
        flops=frames * 1_000_000_000, bytes_accessed=frames * 4_000_000, transcendentals=0
    )


def own_kernel(dims, where, frame, gains, space, time, conv, bands, table, act):
    tiles, width = dims
    build_bands(space, bands)
    build_table(time, table, where[0] == 1)
    normed_conv(frame, act, bands[0], gains[0:1], conv, tiles, width)
    conv[:, lane_tile(tiles)] = frame[:, lane_tile(tiles)]


def own_call(where, frame, gains, space, time):
    height, columns = frame.shape
    width = space.shape[-1]
    tiles = columns // LANES - 1
    return pl.pallas_call(
        functools.partial(own_kernel, (tiles, width)),
        out_shape=(
            like(frame),
            jax.ShapeDtypeStruct((BLOCKS, 4 * width, 3 * LANES), jnp.bfloat16),
            jax.ShapeDtypeStruct((BLOCKS, TIME_TAPS + 2, LANES, LANES), jnp.bfloat16),
        ),
        in_specs=[pl.BlockSpec(memory_space=pltpu.SMEM)] + [WHOLE] * 4,
        out_specs=(WHOLE,) * 3,
        scratch_shapes=act_scratch(height, columns),
        compiler_params=pltpu.CompilerParams(vmem_limit_bytes=GRANT),
        cost_estimate=estimate(1),
        name="own",
    )(where, frame, gains, space, time)


def next_kernel(dims, where, outer, inner, gains, bands, xn, sn, xo, so, act, sem):
    tiles, width = dims
    middle = where[1] == 1

    def conv(result, frame):
        normed_conv(frame, act, bands[0], gains[0:1], result, tiles, width)
        result[:, lane_tile(tiles)] = frame[:, lane_tile(tiles)]

    @pl.when(jnp.logical_not(middle))
    def _():
        fetch(outer, xn, sem)
        so[...] = jnp.zeros(so.shape, so.dtype)

    @pl.when(middle)
    def _():
        fetch(outer, xo, sem)
        conv(so, xo)
        fetch(inner, xn, sem)

    conv(sn, xn)


def next_call(where, outer, inner, gains, bands):
    height, columns = outer.shape
    tiles, width = columns // LANES - 1, gains.shape[-1]
    return pl.pallas_call(
        functools.partial(next_kernel, (tiles, width)),
        out_shape=(like(outer),) * 4,
        in_specs=[pl.BlockSpec(memory_space=pltpu.SMEM), PLACED, PLACED, WHOLE, WHOLE],
        out_specs=(WHOLE,) * 4,
        scratch_shapes=act_scratch(height, columns) + [pltpu.SemaphoreType.DMA],
        compiler_params=pltpu.CompilerParams(vmem_limit_bytes=GRANT),
        cost_estimate=estimate(2),
        name="next",
    )(where, outer, inner, gains, bands)


def places(middle, target):
    one = middle.astype(jnp.int32)
    lie = [one, one + 1, one + 2, 3 - 3 * one]
    return [at - lie[target] + REACH + 1 for at in lie]


def clamped(entries):
    return [jnp.clip(entry, 0, TIME_TAPS + 1) for entry in entries]


def weights_of(table, sources, middle, tiles, targets, kept):
    marks = [mark_of(source, tiles) for source in sources]

    def column(target):
        entries = clamped(places(middle, target))
        chosen = [marks[place] for place in kept], [entries[place] for place in kept]
        return marked_weights(table, chosen[0], marks[target], chosen[1])

    return jnp.concatenate([column(target) for target in targets], 1)


def after_kernel(dims, *refs):
    tiles, width = dims
    where, xa, gains, bands, table, xs, ss, sn, xo, so = refs[:10]
    sa, xs1, sums = refs[10:13]
    act, x1, ss1, so1 = refs[13:]
    middle = where[1] == 1

    normed_conv(xa, act, bands[0], gains[0:1], sa, tiles, width)
    sa[:, lane_tile(tiles)] = xa[:, lane_tile(tiles)]

    sources = (ss, sn, sa, so)
    weights = weights_of(table.at[0], sources, middle, tiles, (0, 3), (0, 1, 2, 3))
    temporal(sources, weights, tiles, adding((xs, xo), (xs1, x1)))
    normed_conv(xs1, act, bands[1], gains[1:2], ss1, tiles, width)

    @pl.when(jnp.logical_not(middle))
    def _():
        so1[...] = jnp.zeros(so1.shape, so1.dtype)

    pl.when(middle)(lambda: normed_conv(x1, act, bands[1], gains[1:2], so1, tiles, width))

    def keep(at, target, total):
        sums[:, at] = total

    weights = weights_of(table.at[1], sources, middle, tiles, (0,), (0, 3))
    temporal((ss1, so1), weights, tiles, keep)


def after_call(where, xa, gains, bands, table, xs, ss, sn, xo, so):
    height, columns = xs.shape
    tiles, width = columns // LANES - 1, gains.shape[-1]
    plain = pltpu.VMEM((height, columns - LANES), jnp.bfloat16)
    return pl.pallas_call(
        functools.partial(after_kernel, (tiles, width)),
        out_shape=(
            like(xs),
            like(xs, -LANES),
            jax.ShapeDtypeStruct((height, columns - LANES), jnp.float32),
        ),
        in_specs=[pl.BlockSpec(memory_space=pltpu.SMEM)] + [WHOLE] * 9,
        out_specs=(WHOLE,) * 3,
        scratch_shapes=act_scratch(height, columns) + [plain] * 3,
        compiler_params=pltpu.CompilerParams(vmem_limit_bytes=GRANT),
        cost_estimate=estimate(2),
        name="after",
    )(where, xa, gains, bands, table, xs, ss, sn, xo, so)


def last_kernel(dims, *refs):
    tiles, width = dims
    where, corner, gains, bands, table, ss, sn, so_mid, sa, xn, xa, xs1, sums = refs[:13]
    out = refs[13]
    act, so, xn1, xa1, sn1, sa1, sem = refs[14:]
    middle = where[1] == 1

    pl.when(middle)(lambda: fetch(so_mid, so, sem))
    pl.when(jnp.logical_not(middle))(lambda: fetch(corner, so, sem))
    sources = (ss, sn, sa, so)
    weights = weights_of(table.at[0], sources, middle, tiles, (1, 2), (0, 1, 2, 3))
    temporal(sources, weights, tiles, adding((xn, xa), (xn1, xa1)))
    normed_conv(xn1, act, bands[1], gains[1:2], sn1, tiles, width)
    normed_conv(xa1, act, bands[1], gains[1:2], sa1, tiles, width)

    def finish(at, target, total):
        update = (sums[:, at] + total).astype(jnp.bfloat16).astype(jnp.float32)
        out[0, :, at] = (xs1[:, at].astype(jnp.float32) + update).astype(jnp.bfloat16)

    weights = weights_of(table.at[1], sources, middle, tiles, (0,), (1, 2))
    temporal((sn1, sa1), weights, tiles, finish)


def last_call(where, corner, gains, bands, table, ss, sn, so, sa, xn, xa, xs1, sums):
    height, columns = xn.shape
    tiles, width = columns // LANES - 1, gains.shape[-1]
    plain = pltpu.VMEM((height, columns - LANES), jnp.bfloat16)
    return pl.pallas_call(
        functools.partial(last_kernel, (tiles, width)),
        out_shape=jax.ShapeDtypeStruct((1, height, columns - LANES), jnp.bfloat16),
        in_specs=[pl.BlockSpec(memory_space=pltpu.SMEM), PLACED] + [WHOLE] * 11,
        out_specs=WHOLE,
        scratch_shapes=act_scratch(height, columns)
        + [pltpu.VMEM((height, columns), jnp.bfloat16)]
        + [plain] * 4
        + [pltpu.SemaphoreType.DMA],
        compiler_params=pltpu.CompilerParams(vmem_limit_bytes=GRANT),
        cost_estimate=estimate(3),
        name="last",
    )(where, corner, gains, bands, table, ss, sn, so, sa, xn, xa, xs1, sums)


def moved(values, hops):
    pairs = [(TIME_DILATION * a + c, TIME_DILATION * b + c) for a, b in hops for c in (0, 1)]
    return lax.ppermute(values, "dev", pairs)


def on_a_line(frames, clip_ids, norm_gain, space_kernel, time_kernel):
    chip = lax.axis_index("dev") // TIME_DILATION
    near, middle = chip < 2, (chip == 1) | (chip == 2)
    where = jnp.stack([near, middle]).astype(jnp.int32)
    xs = mark_frames(frames, clip_ids)
    outer = moved(xs, [(0, 1), (1, 0), (2, 3), (3, 2)])
    inner = moved(xs, [(0, 0), (1, 2), (2, 1), (3, 3)])
    ss, bands, table = own_call(where, xs, norm_gain, space_kernel, time_kernel)
    outer, _ = lax.optimization_barrier((outer, ss))
    inner, _ = lax.optimization_barrier((inner, outer))
    after = moved(inner, [(0, 2), (1, 0), (2, 3), (3, 1)])
    xn, sn, xo, so = next_call(where, outer, inner, norm_gain, bands)
    sent, _ = lax.optimization_barrier((ss, sn))
    corner = moved(sent, [(0, 3), (1, 1), (2, 2), (3, 0)])
    sa, xs1, sums = after_call(where, after, norm_gain, bands, table, xs, ss, sn, xo, so)
    return last_call(where, corner, norm_gain, bands, table, ss, sn, so, sa, xn, after, xs1, sums)


def conv_kernel(dims, block, frame, gains, bands, conv, act):
    tiles, width = dims
    normed_conv(frame, act, bands[block], gains[block : block + 1], conv, tiles, width)
    conv[:, lane_tile(tiles)] = frame[:, lane_tile(tiles)]


def conv_call(block, frame, gains, bands):
    height, columns = frame.shape
    tiles, width = columns // LANES - 1, gains.shape[-1]
    return pl.pallas_call(
        functools.partial(conv_kernel, (tiles, width), block),
        out_shape=like(frame),
        in_specs=[WHOLE] * 3,
        out_specs=WHOLE,
        scratch_shapes=act_scratch(height, columns),
        compiler_params=pltpu.CompilerParams(vmem_limit_bytes=GRANT),
        name="conv",
    )(frame, gains, bands)


def mix_kernel(tiles, block, frame, table, *refs):
    sources, result = refs[:TIME_TAPS], refs[TIME_TAPS]
    marks = [mark_of(source, tiles) for source in sources]
    entries = range(1, TIME_TAPS + 1)
    weights = marked_weights(table.at[block], marks, marks[REACH], entries)
    temporal(sources, weights, tiles, adding([frame], [result]))
    result[:, lane_tile(tiles)] = frame[:, lane_tile(tiles)]


def mix_call(block, frame, table, sources):
    return pl.pallas_call(
        functools.partial(mix_kernel, frame.shape[1] // LANES - 1, block),
        out_shape=like(frame),
        in_specs=[WHOLE] * (2 + TIME_TAPS),
        out_specs=WHOLE,
        compiler_params=pltpu.CompilerParams(vmem_limit_bytes=GRANT),
        name="mix",
    )(frame, table, *sources)


def by_relays(frames, clip_ids, norm_gain, space_kernel, time_kernel):
    chips = lax.axis_size("dev") // TIME_DILATION
    up = [(i, i + 1) for i in range(chips - 1)]
    down = [(i + 1, i) for i in range(chips - 1)]
    frame = mark_frames(frames, clip_ids)
    where = jnp.ones((2,), jnp.int32)
    conv, bands, table = own_call(where, frame, norm_gain, space_kernel, time_kernel)
    for block in range(BLOCKS):
        if block > 0:
            conv = conv_call(block, frame, norm_gain, bands)
        sources = [conv]
        for _ in range(REACH):
            sources = [moved(sources[0], up)] + sources + [moved(sources[-1], down)]
        frame = mix_call(block, frame, table, sources)
    return frame[None, :, : frames.shape[2]]


def per_device(*args):
    return (on_a_line if lax.axis_size("dev") == 8 else by_relays)(*args)


def solution(mesh):
    return jax.shard_map(
        per_device,
        mesh=mesh,
        in_specs=(P(("dp", "dev"), None, None), P(("dp", "dev")), P(), P(), P()),
        out_specs=P(("dp", "dev"), None, None),
        check_vma=False,
    )
```

time: 94.6 us -> 72.4 us (0.77)
  the two profiles are of different devices: /device:TPU:16 before, /device:TPU:0 now
where the time goes in v2:
time: 72.4 us; the launch traced here: 72.2 us
  waiting for transfers between devices  35.3 us (49%)
  Pallas kernels  22.1 us (31%)
  starting transfers between devices  12.8 us (18%)
  local copies, waits for them, and re-layouts  1.14 us (2%)
  between operations  0.75 us (1%)
    ppermute x4, waiting for transfers between devices, moved(): return lax.ppermute(values, 'dev', pairs)  35.3 us
    ppermute x4, starting transfers between devices, moved(): return lax.ppermute(values, 'dev', pairs)  12.8 us
    pallas_call x1, Pallas kernels, last_call(): pl.pallas_call(functools.partial(last_kernel, (tiles, width)), out_shape=...  8.51 us
    pallas_call x1, Pallas kernels, after_call(): pl.pallas_call(functools.partial(after_kernel, (tiles, width)), out_shape...  7.42 us
    pallas_call x1, Pallas kernels, next_call(): pl.pallas_call(functools.partial(next_kernel, (tiles, width)), out_shape=...  3.07 us
    pallas_call x1, Pallas kernels, own_call(): pl.pallas_call(functools.partial(own_kernel, (tiles, width)), out_shape=(...  3.01 us
  transfers between devices with their start and end apart: 4, of which 3 were waited for; matrix products, arithmetic and copies ran while one was open for 0% of the time, Pallas kernels for 19%

profile of v2, /device:TPU:0, one launch (start us, length us, event | category | flops | bytes accessed | tf_op | source)
XLA Modules:
  0.0 72.2 jit_solution(5057714495546011996)
XLA Ops:
  0.0 0.0 copy-start.3
  0.7 0.0 copy-start
  0.7 1.1 %copy-done = bf16[1,48,8192]{2,1,0:T(8,128)(2,1)S(1)} copy-done((bf16[1,48,8192]{2,1,0:T(8,128)(2,1)S(1)}, bf16[1,48,8192]{2,1,0:T(8,128)(2,1)}, u32[]{:S(2)}) %copy-start) | copy-done | bytes 786456
  1.8 0.0 copy-start.1
  1.8 0.0 copy-start.2
  1.8 0.1 mark_frames.1.frame.refs_5_
  1.9 3.1 %collective-permute-start = (bf16[48,8320]{1,0:T(8,128)(2,1)S(1)}, bf16[48,8320]{1,0:T(8,128)(2,1)S(1)}, u32[]{:S(2)}, u32[]{:S(2)}) collective-permute-start(bf16[48,8320]{1,0:T(8,128)(2,1)S(1)} %mark_frames.1.frame.refs_5_), channel_id=1, source_target_pairs={{0,2},{1,3},{2,0},{3,1},{4,6},{5,7},{6,4},{7,5},{8,10},{9,11},{10,... | collective-permute-start | bytes 2396168 | tf_op jit(solution)/shard_map/ppermute | solution.py:395
  5.0 0.7 collective-permute-start.1
  5.8 0.1 add_convert_fusion.where.refs_0_
  5.8 0.0 copy-done.3
  5.8 0.0 copy-done.1
  5.8 0.0 copy-done.2
  5.8 3.0 %own.1 = (bf16[48,8320]{1,0:T(8,128)(2,1)S(1)}, bf16[2,256,384]{2,1,0:T(8,128)(2,1)S(1)}, bf16[2,7,128,128]{3,2,1,0:T(8,128)(2,1)S(1)}) custom-call(s32[2]{0:T(128)S(1)} %add_convert_fusion.where.refs_0_, bf16[48,8320]{1,0:T(8,128)(2,1)S(1)} %mark_frames.1.frame.refs_5_, f32[2,64]{1,0:T(2,128)S(1)} %copy-done.3, bf16[2,3,3,64,64]{4,3,2,1,0:T(8,128)(2,1)S(1)} %copy-done.1, ...), custom_call_target="tpu_custom_call" | custom-call | flops 1000000000 | bytes 4000000 | tf_op jit(solution)/shard_map/own/pallas_call | solution.py:229
  8.9 14.0 %collective-permute-done.outer = bf16[48,8320]{1,0:T(8,128)(2,1)S(1)} collective-permute-done((bf16[48,8320]{1,0:T(8,128)(2,1)S(1)}, bf16[48,8320]{1,0:T(8,128)(2,1)S(1)}, u32[]{:S(2)}, u32[]{:S(2)}) %collective-permute-start) | collective-permute-done | bytes 798752 | tf_op jit(solution)/shard_map/ppermute | solution.py:395
  22.8 0.0 collective-permute-done.1.inner
  22.8 5.9 %collective-permute-start.3 = (bf16[48,8320]{1,0:T(8,128)(2,1)S(1)}, bf16[48,8320]{1,0:T(8,128)(2,1)S(1)}, u32[]{:S(2)}, u32[]{:S(2)}) collective-permute-start(bf16[48,8320]{1,0:T(8,128)(2,1)S(1)} %collective-permute-done.1.inner), channel_id=1, source_target_pairs={{0,4},{1,5},{2,0},{3,1},{4,6},{5,7},{6,2},{7,3},{8,12},{9,13},{10,... | collective-permute-start | bytes 2396168 | tf_op jit(solution)/shard_map/ppermute | solution.py:395
  28.8 3.1 %next.1 = (bf16[48,8320]{1,0:T(8,128)(2,1)S(1)}, bf16[48,8320]{1,0:T(8,128)(2,1)S(1)}, bf16[48,8320]{1,0:T(8,128)(2,1)S(1)}, bf16[48,8320]{1,0:T(8,128)(2,1)S(1)}) custom-call(s32[2]{0:T(128)S(1)} %add_convert_fusion.where.refs_0_, bf16[48,8320]{1,0:T(8,128)(2,1)S(1)} %collective-permute-done.outer, bf16[48,8320]{1,0:T(8,128)(2,1)S(1)} %collective-permute-done.1.inner, ...), custom_call_target="tpu_custom_call" | custom-call | flops 2000000000 | bytes 8000000 | tf_op jit(solution)/shard_map/next/pallas_call | solution.py:270
  31.8 3.1 %collective-permute-start.2 = (bf16[48,8320]{1,0:T(8,128)(2,1)S(1)}, bf16[48,8320]{1,0:T(8,128)(2,1)S(1)}, u32[]{:S(2)}, u32[]{:S(2)}) collective-permute-start(bf16[48,8320]{1,0:T(8,128)(2,1)S(1)} %get-tuple-element.23.refs_6_.refs_5_), channel_id=1, source_target_pairs={{0,6},{1,7},{2,2},{3,3},{4,4},{5,5},{6,0},{7,1},{8,14},{9,15},{10,... | collective-permute-start | bytes 2396168 | tf_op jit(solution)/shard_map/ppermute | solution.py:395
  34.9 12.0 %collective-permute-done.3.refs_1_.refs_10_ = bf16[48,8320]{1,0:T(8,128)(2,1)S(1)} collective-permute-done((bf16[48,8320]{1,0:T(8,128)(2,1)S(1)}, bf16[48,8320]{1,0:T(8,128)(2,1)S(1)}, u32[]{:S(2)}, u32[]{:S(2)}) %collective-permute-start.3) | collective-permute-done | bytes 798752 | tf_op jit(solution)/shard_map/ppermute | solution.py:395
  47.0 7.4 %after.1 = (bf16[48,8320]{1,0:T(8,128)(2,1)S(1)}, bf16[48,8192]{1,0:T(8,128)(2,1)S(1)}, f32[48,8192]{1,0:T(8,128)S(1)}) custom-call(s32[2]{0:T(128)S(1)} %add_convert_fusion.where.refs_0_, bf16[48,8320]{1,0:T(8,128)(2,1)S(1)} %collective-permute-done.3.refs_1_.refs_10_, f32[2,64]{1,0:T(2,128)S(1)} %copy-done.3, ...), custom_call_target="tpu_custom_call" | custom-call | flops 2000000000 | bytes 8000000 | tf_op jit(solution)/shard_map/after/pallas_call | solution.py:335
  54.4 9.3 %collective-permute-done.2.refs_1_ = bf16[48,8320]{1,0:T(8,128)(2,1)S(1)} collective-permute-done((bf16[48,8320]{1,0:T(8,128)(2,1)S(1)}, bf16[48,8320]{1,0:T(8,128)(2,1)S(1)}, u32[]{:S(2)}, u32[]{:S(2)}) %collective-permute-start.2) | collective-permute-done | bytes 798752 | tf_op jit(solution)/shard_map/ppermute | solution.py:395
  63.7 8.5 %last.1 = bf16[1,48,8192]{2,1,0:T(8,128)(2,1)} custom-call(s32[2]{0:T(128)S(1)} %add_convert_fusion.where.refs_0_, bf16[48,8320]{1,0:T(8,128)(2,1)S(1)} %collective-permute-done.2.refs_1_, f32[2,64]{1,0:T(2,128)S(1)} %copy-done.3, bf16[2,256,384]{2,1,0:T(8,128)(2,1)S(1)} %get-tuple-element.21.bands.refs_3_, ...), custom_call_target="tpu_custom_call" | custom-call | flops 3000000000 | bytes 12000000 | tf_op jit(solution)/shard_map/last/pallas_call | solution.py:378
Async XLA Ops:
  0.0 5.8 %copy-start.3 = (f32[2,64]{1,0:T(2,128)S(1)}, f32[2,64]{1,0:T(2,128)}, u32[]{:S(2)}) copy-start(f32[2,64]{1,0:T(2,128)} %refs_2_.3) | copy-start | bytes 1540
  0.7 1.1 %copy-start = (bf16[1,48,8192]{2,1,0:T(8,128)(2,1)S(1)}, bf16[1,48,8192]{2,1,0:T(8,128)(2,1)}, u32[]{:S(2)}) copy-start(bf16[1,48,8192]{2,1,0:T(8,128)(2,1)} %frame.1) | copy-start | bytes 2359300
  1.8 4.0 %copy-start.1 = (bf16[2,3,3,64,64]{4,3,2,1,0:T(8,128)(2,1)S(1)}, bf16[2,3,3,64,64]{4,3,2,1,0:T(8,128)(2,1)}, u32[]{:S(2)}) copy-start(bf16[2,3,3,64,64]{4,3,2,1,0:T(8,128)(2,1)} %space.1) | copy-start | bytes 442372
  1.8 4.0 %copy-start.2 = (bf16[2,5,64,64]{3,2,1,0:T(8,128)(2,1)S(1)}, bf16[2,5,64,64]{3,2,1,0:T(8,128)(2,1)}, u32[]{:S(2)}) copy-start(bf16[2,5,64,64]{3,2,1,0:T(8,128)(2,1)} %time.1) | copy-start | bytes 245764
  1.9 20.9 %collective-permute-start = (bf16[48,8320]{1,0:T(8,128)(2,1)S(1)}, bf16[48,8320]{1,0:T(8,128)(2,1)S(1)}, u32[]{:S(2)}, u32[]{:S(2)}) collective-permute-start(bf16[48,8320]{1,0:T(8,128)(2,1)S(1)} %mark_frames.1.frame.refs_5_), channel_id=1, source_target_pairs={{0,2},{1,3},{2,0},{3,1},{4,6},{5,7},{6,4},{7,5},{8,10},{9,11},{10,... | collective-permute-start | bytes 2396168 | tf_op jit(solution)/shard_map/ppermute | solution.py:395
  5.0 17.8 %collective-permute-start.1 = (bf16[48,8320]{1,0:T(8,128)(2,1)S(1)}, bf16[48,8320]{1,0:T(8,128)(2,1)S(1)}, u32[]{:S(2)}, u32[]{:S(2)}) collective-permute-start(bf16[48,8320]{1,0:T(8,128)(2,1)S(1)} %mark_frames.1.frame.refs_5_), channel_id=1, source_target_pairs={{0,0},{1,1},{2,4},{3,5},{4,2},{5,3},{6,6},{7,7},{8,8},{9,9},{10,12... | collective-permute-start | bytes 2396168 | tf_op jit(solution)/shard_map/ppermute | solution.py:395
  22.8 24.1 %collective-permute-start.3 = (bf16[48,8320]{1,0:T(8,128)(2,1)S(1)}, bf16[48,8320]{1,0:T(8,128)(2,1)S(1)}, u32[]{:S(2)}, u32[]{:S(2)}) collective-permute-start(bf16[48,8320]{1,0:T(8,128)(2,1)S(1)} %collective-permute-done.1.inner), channel_id=1, source_target_pairs={{0,4},{1,5},{2,0},{3,1},{4,6},{5,7},{6,2},{7,3},{8,12},{9,13},{10,... | collective-permute-start | bytes 2396168 | tf_op jit(solution)/shard_map/ppermute | solution.py:395
  31.8 31.9 %collective-permute-start.2 = (bf16[48,8320]{1,0:T(8,128)(2,1)S(1)}, bf16[48,8320]{1,0:T(8,128)(2,1)S(1)}, u32[]{:S(2)}, u32[]{:S(2)}) collective-permute-start(bf16[48,8320]{1,0:T(8,128)(2,1)S(1)} %get-tuple-element.23.refs_6_.refs_5_), channel_id=1, source_target_pairs={{0,6},{1,7},{2,2},{3,3},{4,4},{5,5},{6,0},{7,1},{8,14},{9,15},{10,... | collective-permute-start | bytes 2396168 | tf_op jit(solution)/shard_map/ppermute | solution.py:395

commit v3 on v2

--- a/solution.py
+++ b/solution.py
@@ -214,12 +214,17 @@
     )
 
 
-def own_kernel(dims, where, frame, gains, space, time, conv, bands, table, act):
+def own_kernel(dims, where, frame, gains, space, time, conv, given, bands, table, act):
     tiles, width = dims
     build_bands(space, bands)
     build_table(time, table, where[0] == 1)
     normed_conv(frame, act, bands[0], gains[0:1], conv, tiles, width)
-    conv[:, lane_tile(tiles)] = frame[:, lane_tile(tiles)]
+    core = jnp.full((conv.shape[0] - 16, LANES), where[2].astype(jnp.float32))
+    mark = jnp.concatenate([frame[0:16, lane_tile(tiles)], core.astype(jnp.bfloat16)], 0)
+    conv[:, lane_tile(tiles)] = mark
+    for index in range(tiles // 2):
+        given[:, lane_tile(index)] = conv[:, lane_tile((1 - where[2]) * (tiles // 2) + index)]
+    given[:, lane_tile(tiles // 2)] = mark
 
 
 def own_call(where, frame, gains, space, time):
@@ -230,11 +235,12 @@
         functools.partial(own_kernel, (tiles, width)),
         out_shape=(
             like(frame),
+            like(frame, -(tiles // 2) * LANES),
             jax.ShapeDtypeStruct((BLOCKS, 4 * width, 3 * LANES), jnp.bfloat16),
             jax.ShapeDtypeStruct((BLOCKS, TIME_TAPS + 2, LANES, LANES), jnp.bfloat16),
         ),
         in_specs=[pl.BlockSpec(memory_space=pltpu.SMEM)] + [WHOLE] * 4,
-        out_specs=(WHOLE,) * 3,
+        out_specs=(WHOLE,) * 4,
         scratch_shapes=act_scratch(height, columns),
         compiler_params=pltpu.CompilerParams(vmem_limit_bytes=GRANT),
         cost_estimate=estimate(1),
@@ -242,8 +248,9 @@
     )(where, frame, gains, space, time)
 
 
-def next_kernel(dims, where, outer, inner, gains, bands, xn, sn, xo, so, act, sem):
+def next_kernel(dims, *refs):
     tiles, width = dims
+    where, outer, inner, gains, bands, ss, given, xn, sn, xo, so, half, act, sem = refs
     middle = where[1] == 1
 
     def conv(result, frame):
@@ -254,6 +261,14 @@
     def _():
         fetch(outer, xn, sem)
         so[...] = jnp.zeros(so.shape, so.dtype)
+        near, core = where[0].astype(jnp.float32), where[2].astype(jnp.float32)
+        differ = (mark_of(ss, tiles) != mark_of(given, tiles // 2)).astype(jnp.float32)
+        line = differ * near + (1.0 - differ) * (1.0 - near)
+        mine = jnp.broadcast_to(line, (ss.shape[0], LANES)) == core
+        for index in range(tiles // 2 + 1):
+            place = where[2] * (tiles // 2) + index if index < tiles // 2 else tiles
+            kept = jnp.where(mine, float_tile(ss, place), float_tile(given, index))
+            half[:, lane_tile(index)] = kept.astype(jnp.bfloat16)
 
     @pl.when(middle)
     def _():
@@ -264,19 +279,19 @@
     conv(sn, xn)
 
 
-def next_call(where, outer, inner, gains, bands):
+def next_call(where, outer, inner, gains, bands, ss, given):
     height, columns = outer.shape
     tiles, width = columns // LANES - 1, gains.shape[-1]
     return pl.pallas_call(
         functools.partial(next_kernel, (tiles, width)),
-        out_shape=(like(outer),) * 4,
-        in_specs=[pl.BlockSpec(memory_space=pltpu.SMEM), PLACED, PLACED, WHOLE, WHOLE],
-        out_specs=(WHOLE,) * 4,
+        out_shape=(like(outer),) * 4 + (like(given),),
+        in_specs=[pl.BlockSpec(memory_space=pltpu.SMEM), PLACED, PLACED] + [WHOLE] * 4,
+        out_specs=(WHOLE,) * 5,
         scratch_shapes=act_scratch(height, columns) + [pltpu.SemaphoreType.DMA],
         compiler_params=pltpu.CompilerParams(vmem_limit_bytes=GRANT),
         cost_estimate=estimate(2),
         name="next",
-    )(where, outer, inner, gains, bands)
+    )(where, outer, inner, gains, bands, ss, given)
 
 
 def places(middle, target):
@@ -289,9 +304,7 @@
     return [jnp.clip(entry, 0, TIME_TAPS + 1) for entry in entries]
 
 
-def weights_of(table, sources, middle, tiles, targets, kept):
-    marks = [mark_of(source, tiles) for source in sources]
-
+def weights_of(table, marks, middle, targets, kept):
     def column(target):
         entries = clamped(places(middle, target))
         chosen = [marks[place] for place in kept], [entries[place] for place in kept]
@@ -311,7 +324,8 @@
     sa[:, lane_tile(tiles)] = xa[:, lane_tile(tiles)]
 
     sources = (ss, sn, sa, so)
-    weights = weights_of(table.at[0], sources, middle, tiles, (0, 3), (0, 1, 2, 3))
+    marks = [mark_of(source, tiles) for source in sources]
+    weights = weights_of(table.at[0], marks, middle, (0, 3), (0, 1, 2, 3))
     temporal(sources, weights, tiles, adding((xs, xo), (xs1, x1)))
     normed_conv(xs1, act, bands[1], gains[1:2], ss1, tiles, width)
 
@@ -324,7 +338,7 @@
     def keep(at, target, total):
         sums[:, at] = total
 
-    weights = weights_of(table.at[1], sources, middle, tiles, (0,), (0, 3))
+    weights = weights_of(table.at[1], marks, middle, (0,), (0, 3))
     temporal((ss1, so1), weights, tiles, keep)
 
 
@@ -350,15 +364,33 @@
 
 def last_kernel(dims, *refs):
     tiles, width = dims
-    where, corner, gains, bands, table, ss, sn, so_mid, sa, xn, xa, xs1, sums = refs[:13]
-    out = refs[13]
-    act, so, xn1, xa1, sn1, sa1, sem = refs[14:]
+    where, mine, given, gains, bands, table, ss, sn, so_mid, sa, xn, xa, xs1, sums = refs[:14]
+    out = refs[14]
+    act, so, xn1, xa1, sn1, sa1, sem = refs[15:]
     middle = where[1] == 1
 
-    pl.when(middle)(lambda: fetch(so_mid, so, sem))
-    pl.when(jnp.logical_not(middle))(lambda: fetch(corner, so, sem))
+    pl.when(middle)(lambda: fetch(so_mid, so, sem.at[0]))
+
+    @pl.when(jnp.logical_not(middle))
+    def _():
+        part = tiles // 2
+        copies = [
+            (mine.at[:, lane_tile(0, part)], so.at[:, lane_tile(where[2] * part, part)]),
+            (given.at[:, lane_tile(0, part)], so.at[:, lane_tile((1 - where[2]) * part, part)]),
+            (mine.at[:, lane_tile(part)], so.at[:, lane_tile(tiles)]),
+        ]
+        copies = [pltpu.make_async_copy(*ends, sem.at[i]) for i, ends in enumerate(copies)]
+        for copy in copies:
+            copy.start()
+        for copy in copies:
+            copy.wait()
+
     sources = (ss, sn, sa, so)
-    weights = weights_of(table.at[0], sources, middle, tiles, (1, 2), (0, 1, 2, 3))
+    marks = [mark_of(source, tiles) for source in sources]
+    core = so[16:32, lane_tile(tiles)].astype(jnp.float32)[:1]
+    valid = jnp.logical_or(core == where[2].astype(jnp.float32), middle)
+    marks[3] = jnp.where(valid, marks[3], -1.0)
+    weights = weights_of(table.at[0], marks, middle, (1, 2), (0, 1, 2, 3))
     temporal(sources, weights, tiles, adding((xn, xa), (xn1, xa1)))
     normed_conv(xn1, act, bands[1], gains[1:2], sn1, tiles, width)
     normed_conv(xa1, act, bands[1], gains[1:2], sa1, tiles, width)
@@ -367,50 +399,59 @@
         update = (sums[:, at] + total).astype(jnp.bfloat16).astype(jnp.float32)
         out[0, :, at] = (xs1[:, at].astype(jnp.float32) + update).astype(jnp.bfloat16)
 
-    weights = weights_of(table.at[1], sources, middle, tiles, (0,), (1, 2))
+    weights = weights_of(table.at[1], marks, middle, (0,), (1, 2))
     temporal((sn1, sa1), weights, tiles, finish)
 
 
-def last_call(where, corner, gains, bands, table, ss, sn, so, sa, xn, xa, xs1, sums):
+def last_call(where, mine, given, gains, bands, table, ss, sn, so, sa, xn, xa, xs1, sums):
     height, columns = xn.shape
     tiles, width = columns // LANES - 1, gains.shape[-1]
     plain = pltpu.VMEM((height, columns - LANES), jnp.bfloat16)
     return pl.pallas_call(
         functools.partial(last_kernel, (tiles, width)),
         out_shape=jax.ShapeDtypeStruct((1, height, columns - LANES), jnp.bfloat16),
-        in_specs=[pl.BlockSpec(memory_space=pltpu.SMEM), PLACED] + [WHOLE] * 11,
+        in_specs=[pl.BlockSpec(memory_space=pltpu.SMEM)] + [PLACED] * 2 + [WHOLE] * 11,
         out_specs=WHOLE,
         scratch_shapes=act_scratch(height, columns)
         + [pltpu.VMEM((height, columns), jnp.bfloat16)]
         + [plain] * 4
-        + [pltpu.SemaphoreType.DMA],
+        + [pltpu.SemaphoreType.DMA((3,))],
         compiler_params=pltpu.CompilerParams(vmem_limit_bytes=GRANT),
         cost_estimate=estimate(3),
         name="last",
-    )(where, corner, gains, bands, table, ss, sn, so, sa, xn, xa, xs1, sums)
-
-
-def moved(values, hops):
-    pairs = [(TIME_DILATION * a + c, TIME_DILATION * b + c) for a, b in hops for c in (0, 1)]
+    )(where, mine, given, gains, bands, table, ss, sn, so, sa, xn, xa, xs1, sums)
+
+
+def moved(values, hops, swap=()):
+    pairs = []
+    for a, b in hops:
+        for core in range(TIME_DILATION):
+            target = TIME_DILATION - 1 - core if a in swap else core
+            pairs.append((TIME_DILATION * a + core, TIME_DILATION * b + target))
     return lax.ppermute(values, "dev", pairs)
 
 
 def on_a_line(frames, clip_ids, norm_gain, space_kernel, time_kernel):
-    chip = lax.axis_index("dev") // TIME_DILATION
+    device = lax.axis_index("dev")
+    chip = device // TIME_DILATION
     near, middle = chip < 2, (chip == 1) | (chip == 2)
-    where = jnp.stack([near, middle]).astype(jnp.int32)
+    where = jnp.stack([near, middle, device % TIME_DILATION == 1]).astype(jnp.int32)
     xs = mark_frames(frames, clip_ids)
     outer = moved(xs, [(0, 1), (1, 0), (2, 3), (3, 2)])
     inner = moved(xs, [(0, 0), (1, 2), (2, 1), (3, 3)])
-    ss, bands, table = own_call(where, xs, norm_gain, space_kernel, time_kernel)
-    outer, _ = lax.optimization_barrier((outer, ss))
+    ss, given, bands, table = own_call(where, xs, norm_gain, space_kernel, time_kernel)
+    given = moved(given, [(chip, chip) for chip in range(4)], swap=range(4))
+    outer, _ = lax.optimization_barrier((outer, given))
     inner, _ = lax.optimization_barrier((inner, outer))
     after = moved(inner, [(0, 2), (1, 0), (2, 3), (3, 1)])
-    xn, sn, xo, so = next_call(where, outer, inner, norm_gain, bands)
-    sent, _ = lax.optimization_barrier((ss, sn))
-    corner = moved(sent, [(0, 3), (1, 1), (2, 2), (3, 0)])
+    xn, sn, xo, so, half = next_call(where, outer, inner, norm_gain, bands, ss, given)
+    mine = moved(half, [(0, 3), (1, 1), (2, 2), (3, 0)])
     sa, xs1, sums = after_call(where, after, norm_gain, bands, table, xs, ss, sn, xo, so)
-    return last_call(where, corner, norm_gain, bands, table, ss, sn, so, sa, xn, after, xs1, sums)
+    mine, _ = lax.optimization_barrier((mine, sums))
+    given = moved(mine, [(chip, chip) for chip in range(4)], swap=(0, 3))
+    return last_call(
+        where, mine, given, norm_gain, bands, table, ss, sn, so, sa, xn, after, xs1, sums
+    )
 
 
 def conv_kernel(dims, block, frame, gains, bands, conv, act):
@@ -458,8 +499,8 @@
     up = [(i, i + 1) for i in range(chips - 1)]
     down = [(i + 1, i) for i in range(chips - 1)]
     frame = mark_frames(frames, clip_ids)
-    where = jnp.ones((2,), jnp.int32)
-    conv, bands, table = own_call(where, frame, norm_gain, space_kernel, time_kernel)
+    where = jnp.array([1, 0, 0], jnp.int32)
+    conv, _, bands, table = own_call(where, frame, norm_gain, space_kernel, time_kernel)
     for block in range(BLOCKS):
         if block > 0:
             conv = conv_call(block, frame, norm_gain, bands)

time: 72.4 us -> 67.7 us (0.935)
  waiting for transfers between devices: 35.3 us -> 28.3 us
  starting transfers between devices: 12.8 us -> 14.8 us
    ppermute x4 -> x6, waiting for transfers between devices: 35.3 us -> 28.3 us  [moved(): return lax.ppermute(values, 'dev', pairs)]
    ppermute x4 -> x6, starting transfers between devices: 12.8 us -> 14.8 us  [moved(): return lax.ppermute(values, 'dev', pairs)]
  transfers between devices with their start and end apart: 4 -> 6, of which waited for: 3 -> 5; matrix products, arithmetic and copies ran while one was open for 0% -> 0% of each run, Pallas kernels for 19% -> 20%
where the time goes in v3:
time: 67.7 us; the launch traced here: 67.5 us
  waiting for transfers between devices  28.3 us (42%)
  Pallas kernels  22.3 us (33%)
  starting transfers between devices  14.8 us (22%)
  local copies, waits for them, and re-layouts  1.14 us (2%)
  between operations  0.77 us (1%)
    ppermute x6, waiting for transfers between devices, moved(): return lax.ppermute(values, 'dev', pairs)  28.3 us
    ppermute x6, starting transfers between devices, moved(): return lax.ppermute(values, 'dev', pairs)  14.8 us
    pallas_call x1, Pallas kernels, last_call(): pl.pallas_call(functools.partial(last_kernel, (tiles, width)), out_shape=...  8.53 us
    pallas_call x1, Pallas kernels, after_call(): pl.pallas_call(functools.partial(after_kernel, (tiles, width)), out_shape...  7.42 us
    pallas_call x1, Pallas kernels, next_call(): pl.pallas_call(functools.partial(next_kernel, (tiles, width)), out_shape=...  3.16 us
    pallas_call x1, Pallas kernels, own_call(): pl.pallas_call(functools.partial(own_kernel, (tiles, width)), out_shape=(...  3.09 us
  transfers between devices with their start and end apart: 6, of which 5 were waited for; matrix products, arithmetic and copies ran while one was open for 0% of the time, Pallas kernels for 20%

profile of v3, /device:TPU:0, one launch (start us, length us, event | category | flops | bytes accessed | tf_op | source)
XLA Modules:
  0.0 67.5 jit_solution(10261201774036420005)
XLA Ops:
  0.0 0.0 copy-start.3
  0.7 0.0 copy-start
  0.7 1.1 %copy-done = bf16[1,48,8192]{2,1,0:T(8,128)(2,1)S(1)} copy-done((bf16[1,48,8192]{2,1,0:T(8,128)(2,1)S(1)}, bf16[1,48,8192]{2,1,0:T(8,128)(2,1)}, u32[]{:S(2)}) %copy-start) | copy-done | bytes 786456
  1.8 0.0 copy-start.1
  1.8 0.0 copy-start.2
  1.8 0.1 mark_frames.1.frame.refs_5_
  1.9 3.1 %collective-permute-start = (bf16[48,8320]{1,0:T(8,128)(2,1)S(1)}, bf16[48,8320]{1,0:T(8,128)(2,1)S(1)}, u32[]{:S(2)}, u32[]{:S(2)}) collective-permute-start(bf16[48,8320]{1,0:T(8,128)(2,1)S(1)} %mark_frames.1.frame.refs_5_), channel_id=1, source_target_pairs={{0,2},{1,3},{2,0},{3,1},{4,6},{5,7},{6,4},{7,5},{8,10},{9,11},{10,... | collective-permute-start | bytes 2396168 | tf_op jit(solution)/shard_map/ppermute | solution.py:431
  5.0 0.7 %collective-permute-start.2 = (bf16[48,8320]{1,0:T(8,128)(2,1)S(1)}, bf16[48,8320]{1,0:T(8,128)(2,1)S(1)}, u32[]{:S(2)}, u32[]{:S(2)}) collective-permute-start(bf16[48,8320]{1,0:T(8,128)(2,1)S(1)} %mark_frames.1.frame.refs_5_), channel_id=1, source_target_pairs={{0,0},{1,1},{2,4},{3,5},{4,2},{5,3},{6,6},{7,7},{8,8},{9,9},{10,12... | collective-permute-start | bytes 2396168 | tf_op jit(solution)/shard_map/ppermute | solution.py:431
  5.8 0.1 add_convert_fusion.where.refs_0_
  5.8 0.0 copy-done.3
  5.8 0.0 copy-done.1
  5.8 0.0 copy-done.2
  5.8 3.1 %own.1 = (bf16[48,8320]{1,0:T(8,128)(2,1)S(1)}, bf16[48,4224]{1,0:T(8,128)(2,1)S(1)}, bf16[2,256,384]{2,1,0:T(8,128)(2,1)S(1)}, bf16[2,7,128,128]{3,2,1,0:T(8,128)(2,1)S(1)}) custom-call(s32[3]{0:T(128)S(1)} %add_convert_fusion.where.refs_0_, bf16[48,8320]{1,0:T(8,128)(2,1)S(1)} %mark_frames.1.frame.refs_5_, f32[2,64]{1,0:T(2,128)S(1)} %copy-done.3, ...), custom_call_target="tpu_custom_call" | custom-call | flops 1000000000 | bytes 4000000 | tf_op jit(solution)/shard_map/own/pallas_call | solution.py:234
  8.9 0.1 collective-permute-start.1
  9.0 1.7 %collective-permute-done.1.refs_6_ = bf16[48,4224]{1,0:T(8,128)(2,1)S(1)} collective-permute-done((bf16[48,4224]{1,0:T(8,128)(2,1)S(1)}, bf16[48,4224]{1,0:T(8,128)(2,1)S(1)}, u32[]{:S(2)}, u32[]{:S(2)}) %collective-permute-start.1) | collective-permute-done | bytes 405536 | tf_op jit(solution)/shard_map/ppermute | solution.py:431
  10.7 12.1 %collective-permute-done.refs_1_ = bf16[48,8320]{1,0:T(8,128)(2,1)S(1)} collective-permute-done((bf16[48,8320]{1,0:T(8,128)(2,1)S(1)}, bf16[48,8320]{1,0:T(8,128)(2,1)S(1)}, u32[]{:S(2)}, u32[]{:S(2)}) %collective-permute-start) | collective-permute-done | bytes 798752 | tf_op jit(solution)/shard_map/ppermute | solution.py:431
  22.8 0.0 collective-permute-done.2.refs_2_
  22.8 5.9 %collective-permute-start.4 = (bf16[48,8320]{1,0:T(8,128)(2,1)S(1)}, bf16[48,8320]{1,0:T(8,128)(2,1)S(1)}, u32[]{:S(2)}, u32[]{:S(2)}) collective-permute-start(bf16[48,8320]{1,0:T(8,128)(2,1)S(1)} %collective-permute-done.2.refs_2_), channel_id=1, source_target_pairs={{0,4},{1,5},{2,0},{3,1},{4,6},{5,7},{6,2},{7,3},{8,12},{9,13},{10,... | collective-permute-start | bytes 2396168 | tf_op jit(solution)/shard_map/ppermute | solution.py:431
  28.8 3.2 %next.1 = (bf16[48,8320]{1,0:T(8,128)(2,1)S(1)}, bf16[48,8320]{1,0:T(8,128)(2,1)S(1)}, bf16[48,8320]{1,0:T(8,128)(2,1)S(1)}, bf16[48,8320]{1,0:T(8,128)(2,1)S(1)}, bf16[48,4224]{1,0:T(8,128)(2,1)S(1)}) custom-call(s32[3]{0:T(128)S(1)} %add_convert_fusion.where.refs_0_, bf16[48,8320]{1,0:T(8,128)(2,1)S(1)} %collective-permute-done.refs_1_, ...), custom_call_target="tpu_custom_call" | custom-call | flops 2000000000 | bytes 8000000 | tf_op jit(solution)/shard_map/next/pallas_call | solution.py:285
  31.9 3.1 %collective-permute-start.3 = (bf16[48,4224]{1,0:T(8,128)(2,1)S(1)}, bf16[48,4224]{1,0:T(8,128)(2,1)S(1)}, u32[]{:S(2)}, u32[]{:S(2)}) collective-permute-start(bf16[48,4224]{1,0:T(8,128)(2,1)S(1)} %get-tuple-element.25), channel_id=1, source_target_pairs={{0,6},{1,7},{2,2},{3,3},{4,4},{5,5},{6,0},{7,1},{8,14},{9,15},{10,... | collective-permute-start | bytes 1216520 | tf_op jit(solution)/shard_map/ppermute | solution.py:431
  35.0 11.9 %collective-permute-done.4.refs_1_.refs_11_ = bf16[48,8320]{1,0:T(8,128)(2,1)S(1)} collective-permute-done((bf16[48,8320]{1,0:T(8,128)(2,1)S(1)}, bf16[48,8320]{1,0:T(8,128)(2,1)S(1)}, u32[]{:S(2)}, u32[]{:S(2)}) %collective-permute-start.4) | collective-permute-done | bytes 798752 | tf_op jit(solution)/shard_map/ppermute | solution.py:431
  47.0 7.4 %after.1 = (bf16[48,8320]{1,0:T(8,128)(2,1)S(1)}, bf16[48,8192]{1,0:T(8,128)(2,1)S(1)}, f32[48,8192]{1,0:T(8,128)S(1)}) custom-call(s32[3]{0:T(128)S(1)} %add_convert_fusion.where.refs_0_, bf16[48,8320]{1,0:T(8,128)(2,1)S(1)} %collective-permute-done.4.refs_1_.refs_11_, f32[2,64]{1,0:T(2,128)S(1)} %copy-done.3, ...), custom_call_target="tpu_custom_call" | custom-call | flops 2000000000 | bytes 8000000 | tf_op jit(solution)/shard_map/after/pallas_call | solution.py:349
  54.4 0.9 %collective-permute-done.3.refs_1_ = bf16[48,4224]{1,0:T(8,128)(2,1)S(1)} collective-permute-done((bf16[48,4224]{1,0:T(8,128)(2,1)S(1)}, bf16[48,4224]{1,0:T(8,128)(2,1)S(1)}, u32[]{:S(2)}, u32[]{:S(2)}) %collective-permute-start.3) | collective-permute-done | bytes 405536 | tf_op jit(solution)/shard_map/ppermute | solution.py:431
  55.3 1.9 %collective-permute-start.5 = (bf16[48,4224]{1,0:T(8,128)(2,1)S(1)}, bf16[48,4224]{1,0:T(8,128)(2,1)S(1)}, u32[]{:S(2)}, u32[]{:S(2)}) collective-permute-start(bf16[48,4224]{1,0:T(8,128)(2,1)S(1)} %collective-permute-done.3.refs_1_), channel_id=1, source_target_pairs={{0,1},{1,0},{2,2},{3,3},{4,4},{5,5},{6,7},{7,6},{8,9},{9,8},{10,10... | collective-permute-start | bytes 1216520 | tf_op jit(solution)/shard_map/ppermute | solution.py:431
  57.2 1.7 %collective-permute-done.5.refs_2_ = bf16[48,4224]{1,0:T(8,128)(2,1)S(1)} collective-permute-done((bf16[48,4224]{1,0:T(8,128)(2,1)S(1)}, bf16[48,4224]{1,0:T(8,128)(2,1)S(1)}, u32[]{:S(2)}, u32[]{:S(2)}) %collective-permute-start.5) | collective-permute-done | bytes 405536 | tf_op jit(solution)/shard_map/ppermute | solution.py:431
  58.9 8.5 %last.1 = bf16[1,48,8192]{2,1,0:T(8,128)(2,1)} custom-call(s32[3]{0:T(128)S(1)} %add_convert_fusion.where.refs_0_, bf16[48,4224]{1,0:T(8,128)(2,1)S(1)} %collective-permute-done.3.refs_1_, bf16[48,4224]{1,0:T(8,128)(2,1)S(1)} %collective-permute-done.5.refs_2_, f32[2,64]{1,0:T(2,128)S(1)} %copy-done.3, ...), custom_call_target="tpu_custom_call" | custom-call | flops 3000000000 | bytes 12000000 | tf_op jit(solution)/shard_map/last/pallas_call | solution.py:410
Async XLA Ops:
  0.0 5.8 %copy-start.3 = (f32[2,64]{1,0:T(2,128)S(1)}, f32[2,64]{1,0:T(2,128)}, u32[]{:S(2)}) copy-start(f32[2,64]{1,0:T(2,128)} %refs_3_.3) | copy-start | bytes 1540
  0.7 1.1 %copy-start = (bf16[1,48,8192]{2,1,0:T(8,128)(2,1)S(1)}, bf16[1,48,8192]{2,1,0:T(8,128)(2,1)}, u32[]{:S(2)}) copy-start(bf16[1,48,8192]{2,1,0:T(8,128)(2,1)} %frame.1) | copy-start | bytes 2359300
  1.8 4.0 %copy-start.1 = (bf16[2,3,3,64,64]{4,3,2,1,0:T(8,128)(2,1)S(1)}, bf16[2,3,3,64,64]{4,3,2,1,0:T(8,128)(2,1)}, u32[]{:S(2)}) copy-start(bf16[2,3,3,64,64]{4,3,2,1,0:T(8,128)(2,1)} %space.1) | copy-start | bytes 442372
  1.8 4.0 %copy-start.2 = (bf16[2,5,64,64]{3,2,1,0:T(8,128)(2,1)S(1)}, bf16[2,5,64,64]{3,2,1,0:T(8,128)(2,1)}, u32[]{:S(2)}) copy-start(bf16[2,5,64,64]{3,2,1,0:T(8,128)(2,1)} %time.1) | copy-start | bytes 245764
  1.9 20.9 %collective-permute-start = (bf16[48,8320]{1,0:T(8,128)(2,1)S(1)}, bf16[48,8320]{1,0:T(8,128)(2,1)S(1)}, u32[]{:S(2)}, u32[]{:S(2)}) collective-permute-start(bf16[48,8320]{1,0:T(8,128)(2,1)S(1)} %mark_frames.1.frame.refs_5_), channel_id=1, source_target_pairs={{0,2},{1,3},{2,0},{3,1},{4,6},{5,7},{6,4},{7,5},{8,10},{9,11},{10,... | collective-permute-start | bytes 2396168 | tf_op jit(solution)/shard_map/ppermute | solution.py:431
  5.0 17.8 %collective-permute-start.2 = (bf16[48,8320]{1,0:T(8,128)(2,1)S(1)}, bf16[48,8320]{1,0:T(8,128)(2,1)S(1)}, u32[]{:S(2)}, u32[]{:S(2)}) collective-permute-start(bf16[48,8320]{1,0:T(8,128)(2,1)S(1)} %mark_frames.1.frame.refs_5_), channel_id=1, source_target_pairs={{0,0},{1,1},{2,4},{3,5},{4,2},{5,3},{6,6},{7,7},{8,8},{9,9},{10,12... | collective-permute-start | bytes 2396168 | tf_op jit(solution)/shard_map/ppermute | solution.py:431
  8.9 1.8 %collective-permute-start.1 = (bf16[48,4224]{1,0:T(8,128)(2,1)S(1)}, bf16[48,4224]{1,0:T(8,128)(2,1)S(1)}, u32[]{:S(2)}, u32[]{:S(2)}) collective-permute-start(bf16[48,4224]{1,0:T(8,128)(2,1)S(1)} %get-tuple-element.20), channel_id=1, source_target_pairs={{0,1},{1,0},{2,3},{3,2},{4,5},{5,4},{6,7},{7,6},{8,9},{9,8},{10,11... | collective-permute-start | bytes 1216520 | tf_op jit(solution)/shard_map/ppermute | solution.py:431
  22.8 24.1 %collective-permute-start.4 = (bf16[48,8320]{1,0:T(8,128)(2,1)S(1)}, bf16[48,8320]{1,0:T(8,128)(2,1)S(1)}, u32[]{:S(2)}, u32[]{:S(2)}) collective-permute-start(bf16[48,8320]{1,0:T(8,128)(2,1)S(1)} %collective-permute-done.2.refs_2_), channel_id=1, source_target_pairs={{0,4},{1,5},{2,0},{3,1},{4,6},{5,7},{6,2},{7,3},{8,12},{9,13},{10,... | collective-permute-start | bytes 2396168 | tf_op jit(solution)/shard_map/ppermute | solution.py:431
  31.9 23.4 %collective-permute-start.3 = (bf16[48,4224]{1,0:T(8,128)(2,1)S(1)}, bf16[48,4224]{1,0:T(8,128)(2,1)S(1)}, u32[]{:S(2)}, u32[]{:S(2)}) collective-permute-start(bf16[48,4224]{1,0:T(8,128)(2,1)S(1)} %get-tuple-element.25), channel_id=1, source_target_pairs={{0,6},{1,7},{2,2},{3,3},{4,4},{5,5},{6,0},{7,1},{8,14},{9,15},{10,... | collective-permute-start | bytes 1216520 | tf_op jit(solution)/shard_map/ppermute | solution.py:431
  55.3 3.6 %collective-permute-start.5 = (bf16[48,4224]{1,0:T(8,128)(2,1)S(1)}, bf16[48,4224]{1,0:T(8,128)(2,1)S(1)}, u32[]{:S(2)}, u32[]{:S(2)}) collective-permute-start(bf16[48,4224]{1,0:T(8,128)(2,1)S(1)} %collective-permute-done.3.refs_1_), channel_id=1, source_target_pairs={{0,1},{1,0},{2,2},{3,3},{4,4},{5,5},{6,7},{7,6},{8,9},{9,8},{10,10... | collective-permute-start | bytes 1216520 | tf_op jit(solution)/shard_map/ppermute | solution.py:431

commit v4 on v3

--- a/solution.py
+++ b/solution.py
@@ -6,6 +6,7 @@
 from jax.experimental import pallas as pl
 from jax.experimental.pallas import tpu as pltpu
 from jax.sharding import PartitionSpec as P
+
 
 GROUPS = 32
 TIME_TAPS = 5
@@ -44,47 +45,51 @@
     return jnp.sum(values.reshape(-1, 8, LANES), axis=0)
 
 
-def statistics(frame, tiles, width):
-    share = frame.shape[0] * LANES // GROUPS
-    pivot = fold_groups(by_sublane(float_tile(frame, 0)), width) / share
+def summed(frame, tiles, width):
+    pivot = pivot_of(float_tile(frame, 0), width)
     zero = jnp.zeros((8, LANES), jnp.float32)
 
     def gather(index, totals):
-        shifted = float_tile(frame, index) - pivot
-        return totals[0] + by_sublane(shifted), totals[1] + by_sublane(shifted * shifted)
-
-    sums, squares = lax.fori_loop(0, tiles, gather, (zero, zero), unroll=16)
-    offset = fold_groups(sums, width) / (share * tiles)
-    spread = fold_groups(squares, width) / (share * tiles) - offset * offset
-    return pivot + offset, lax.rsqrt(jnp.maximum(spread, 0.0) + 1e-06)
-
-
-def activate(frame, act, gain, tiles, width):
-    mean, scale = statistics(frame, tiles, width)
-    scale = scale * jnp.concatenate([gain] * (LANES // width), 1) * 0.5
-    height = frame.shape[0]
+        return gathered(float_tile(frame, index), pivot, totals)
+
+    return (pivot, *lax.fori_loop(0, tiles, gather, (zero, zero), unroll=16))
+
+
+def pivot_of(tile, width):
+    return fold_groups(by_sublane(tile), width) / (tile.shape[0] * LANES // GROUPS)
+
+
+def gathered(tile, pivot, totals):
+    shifted = tile - pivot
+    return totals[0] + by_sublane(shifted), totals[1] + by_sublane(shifted * shifted)
+
+
+def scaling(sums, gain, entries, width):
+    pivot, first, second = sums
+    offset = fold_groups(first, width) / entries
+    spread = fold_groups(second, width) / entries - offset * offset
+    scale = lax.rsqrt(jnp.maximum(spread, 0.0) + 1e-06)
+    return pivot + offset, scale * jnp.concatenate([gain] * (LANES // width), 1) * 0.5
+
+
+def convolve(stages, bands, gain, tiles, width):
+    height = stages[0][2].shape[0]
+    pack = tiles
+    entries = height * tiles * LANES // GROUPS
+    row = lax.broadcasted_iota(jnp.int32, (height, LANES), 0)
     lane = lax.broadcasted_iota(jnp.int32, (height, LANES), 1)
 
-    def step(index, last):
-        half = (float_tile(frame, index) - mean) * scale
-        turned = pltpu.roll(half + half * jnp.tanh(half), width, 1)
-        act[:, lane_tile(index)] = jnp.where(lane < width, last, turned).astype(jnp.bfloat16)
-        return turned
-
-    last = lax.fori_loop(0, tiles, step, jnp.zeros((height, LANES), jnp.float32), unroll=16)
-    act[:, lane_tile(tiles)] = jnp.where(lane < width, last, 0.0).astype(jnp.bfloat16)
-
-
-def packed(tiles):
-    return 32 if tiles % 32 == 0 else 1
-
-
-def spatial(act, bands, result, tiles):
-    height = result.shape[0]
-    pack = packed(tiles)
-    row = lax.broadcasted_iota(jnp.int32, (height, LANES), 0)
-
-    def block(first, carry):
+    def activate(stage, first, last):
+        frame, (mean, scale), act = stage
+        for i in range(pack):
+            at = lane_tile(first * pack + i)
+            half = (frame[:, at].astype(jnp.float32) - mean) * scale
+            turned = pltpu.roll(half + half * jnp.tanh(half), width, 1)
+            act[:, at] = jnp.where(lane < width, last, turned).astype(jnp.bfloat16)
+            last = turned
+        return last
+
+    def conv(act, result, first):
         rows = [act[:, lane_tile(first * pack + i, 2)] for i in range(pack)]
         total = jnp.dot(jnp.concatenate(rows, 0), bands, preferred_element_type=jnp.float32)
         for i in range(pack):
@@ -92,21 +97,35 @@
             above = jnp.where(row == 0, 0.0, pltpu.roll(part[:, :LANES], 1, 0))
             below = pltpu.roll(part[:, 2 * LANES :], height - 1, 0)
             below = jnp.where(row == height - 1, 0.0, below)
-            summed = above + part[:, LANES : 2 * LANES] + below
-            result[:, lane_tile(first * pack + i)] = summed.astype(jnp.bfloat16)
-        return carry
-
-    lax.fori_loop(0, tiles // pack, block, 0)
+            sums = above + part[:, LANES : 2 * LANES] + below
+            result[:, lane_tile(first * pack + i)] = sums.astype(jnp.bfloat16)
+
+    before = None
+    for stage in [*stages, None]:
+        now = None
+        if stage is not None:
+            frame, sums, result, act = stage
+            now = frame, scaling(sums, gain, entries, width), act
+
+        def block(first, last, now=now, before=before):
+            if before is not None:
+                conv(*before, first)
+            return last if now is None else activate(now, first, last)
+
+        last = lax.fori_loop(0, tiles // pack, block, jnp.zeros((height, LANES), jnp.float32))
+        before = None
+        if stage is not None:
+            act[:, lane_tile(tiles)] = jnp.where(lane < width, last, 0.0).astype(jnp.bfloat16)
+            before = act, result
 
 
 def normed_conv(frame, act, bands, gain, result, tiles, width):
-    activate(frame, act, gain, tiles, width)
-    spatial(act, bands, result, tiles)
-
-
-def temporal(sources, weights, tiles, emit):
+    convolve([(frame, summed(frame, tiles, width), result, act)], bands, gain, tiles, width)
+
+
+def temporal(sources, weights, tiles, emit, carry=0):
     height = sources[0].shape[0]
-    pack = packed(tiles)
+    pack = tiles
 
     def block(first, carry):
         rows = [
@@ -116,21 +135,51 @@
         total = jnp.dot(jnp.concatenate(rows, 0), weights, preferred_element_type=jnp.float32)
         for i in range(pack):
             part = total[i * height : (i + 1) * height]
-            for target in range(weights.shape[1] // LANES):
-                sums = part[:, target * LANES : (target + 1) * LANES]
-                emit(lane_tile(first * pack + i), target, sums)
+            sums = [part[:, at : at + LANES] for at in range(0, weights.shape[1], LANES)]
+            carry = emit(carry, first, i, lane_tile(first * pack + i), sums)
         return carry
 
-    lax.fori_loop(0, tiles // pack, block, 0)
-
-
-def adding(starts, results):
-    def emit(at, target, sums):
-        update = sums.astype(jnp.bfloat16).astype(jnp.float32)
-        summed = starts[target][:, at].astype(jnp.float32) + update
-        results[target][:, at] = summed.astype(jnp.bfloat16)
-
-    return emit
+    return lax.fori_loop(0, tiles // pack, block, carry)
+
+
+def rounded(start, update):
+    update = update.astype(jnp.bfloat16).astype(jnp.float32)
+    return (start.astype(jnp.float32) + update).astype(jnp.bfloat16)
+
+
+def keep(sources, weights, results, tiles):
+    def emit(carry, first, i, at, sums):
+        for result, total in zip(results, sums):
+            result[:, at] = total
+        return carry
+
+    temporal(sources, weights, tiles, emit)
+
+
+def add_up(start, partial, sources, weights, result, tiles):
+    def emit(carry, first, i, at, sums):
+        result[:, at] = rounded(start[:, at], partial[:, at] + sums[0])
+        return carry
+
+    temporal(sources, weights, tiles, emit)
+
+
+def mix(starts, partials, sources, weights, results, tiles, width):
+    def emit(carry, first, i, at, sums):
+        after = []
+        for place, (pivot, *totals) in enumerate(carry):
+            update = sums[place] if partials is None else sums[place] + partials[place][:, at]
+            added = rounded(starts[place][:, at], update)
+            results[place][:, at] = added
+            added = added.astype(jnp.float32)
+            if i == 0:
+                pivot = jnp.where(first == 0, pivot_of(added, width), pivot)
+            after.append((pivot, *gathered(added, pivot, totals)))
+        return after
+
+    zero = jnp.zeros((8, LANES), jnp.float32)
+    carry = [(zero[:1], zero, zero) for _ in starts]
+    return temporal(sources, weights, tiles, emit, carry)
 
 
 def marked_weights(table, marks, target, places):
@@ -155,9 +204,8 @@
     columns = frame.shape[-1]
     copy = pltpu.make_async_copy(frame.at[0], marked.at[:, pl.ds(0, columns)], sem)
     copy.start()
-    marked[:, columns:] = jnp.full((marked.shape[0], LANES), ids[0].astype(jnp.float32)).astype(
-        jnp.bfloat16
-    )
+    mark = jnp.broadcast_to(ids[...].astype(jnp.float32), (marked.shape[0], LANES))
+    marked[:, columns:] = mark.astype(jnp.bfloat16)
     copy.wait()
 
 
@@ -166,12 +214,12 @@
     return pl.pallas_call(
         mark_kernel,
         out_shape=jax.ShapeDtypeStruct((height, columns + LANES), frames.dtype),
-        in_specs=[pl.BlockSpec(memory_space=pltpu.SMEM), PLACED],
+        in_specs=[WHOLE, PLACED],
         out_specs=WHOLE,
         scratch_shapes=[pltpu.SemaphoreType.DMA],
         compiler_params=pltpu.CompilerParams(vmem_limit_bytes=4 << 20),
         name="mark_frames",
-    )(clip_ids, frames)
+    )(clip_ids[:, None], frames)
 
 
 def build_bands(space, bands):
@@ -316,8 +364,8 @@
 def after_kernel(dims, *refs):
     tiles, width = dims
     where, xa, gains, bands, table, xs, ss, sn, xo, so = refs[:10]
-    sa, xs1, sums = refs[10:13]
-    act, x1, ss1, so1 = refs[13:]
+    sa, xs1, *partial = refs[10:15]
+    act, act_too, x1, ss1, so1 = refs[15:]
     middle = where[1] == 1
 
     normed_conv(xa, act, bands[0], gains[0:1], sa, tiles, width)
@@ -326,36 +374,32 @@
     sources = (ss, sn, sa, so)
     marks = [mark_of(source, tiles) for source in sources]
     weights = weights_of(table.at[0], marks, middle, (0, 3), (0, 1, 2, 3))
-    temporal(sources, weights, tiles, adding((xs, xo), (xs1, x1)))
-    normed_conv(xs1, act, bands[1], gains[1:2], ss1, tiles, width)
+    sums_s, sums_o = mix((xs, xo), None, sources, weights, (xs1, x1), tiles, width)
+    stages = [(xs1, sums_s, ss1, act), (x1, sums_o, so1, act_too)]
 
     @pl.when(jnp.logical_not(middle))
     def _():
         so1[...] = jnp.zeros(so1.shape, so1.dtype)
-
-    pl.when(middle)(lambda: normed_conv(x1, act, bands[1], gains[1:2], so1, tiles, width))
-
-    def keep(at, target, total):
-        sums[:, at] = total
+        convolve(stages[:1], bands[1], gains[1:2], tiles, width)
+
+    pl.when(middle)(lambda: convolve(stages, bands[1], gains[1:2], tiles, width))
 
     weights = weights_of(table.at[1], marks, middle, (0,), (0, 3))
-    temporal((ss1, so1), weights, tiles, keep)
+    keep((ss1, so1), weights, partial[:1], tiles)
+    weights = weights_of(table.at[0], marks, middle, (1, 2), (0, 1, 2))
+    keep((ss, sn, sa), weights, partial[1:], tiles)
 
 
 def after_call(where, xa, gains, bands, table, xs, ss, sn, xo, so):
     height, columns = xs.shape
     tiles, width = columns // LANES - 1, gains.shape[-1]
-    plain = pltpu.VMEM((height, columns - LANES), jnp.bfloat16)
+    partial = jax.ShapeDtypeStruct((height, columns - LANES), jnp.float32)
     return pl.pallas_call(
         functools.partial(after_kernel, (tiles, width)),
-        out_shape=(
-            like(xs),
-            like(xs, -LANES),
-            jax.ShapeDtypeStruct((height, columns - LANES), jnp.float32),
-        ),
+        out_shape=(like(xs), like(xs), partial, partial, partial),
         in_specs=[pl.BlockSpec(memory_space=pltpu.SMEM)] + [WHOLE] * 9,
-        out_specs=(WHOLE,) * 3,
-        scratch_shapes=act_scratch(height, columns) + [plain] * 3,
+        out_specs=(WHOLE,) * 5,
+        scratch_shapes=act_scratch(height, columns) * 5,
         compiler_params=pltpu.CompilerParams(vmem_limit_bytes=GRANT),
         cost_estimate=estimate(2),
         name="after",
@@ -364,9 +408,9 @@
 
 def last_kernel(dims, *refs):
     tiles, width = dims
-    where, mine, given, gains, bands, table, ss, sn, so_mid, sa, xn, xa, xs1, sums = refs[:14]
-    out = refs[14]
-    act, so, xn1, xa1, sn1, sa1, sem = refs[15:]
+    where, mine, given, gains, bands, table, ss, sn, so_mid, sa, xn, xa, xs1 = refs[:13]
+    partial, out = refs[13:16], refs[16]
+    act, act_too, so, xn1, xa1, sn1, sa1, sem = refs[17:]
     middle = where[1] == 1
 
     pl.when(middle)(lambda: fetch(so_mid, so, sem.at[0]))
@@ -390,36 +434,28 @@
     core = so[16:32, lane_tile(tiles)].astype(jnp.float32)[:1]
     valid = jnp.logical_or(core == where[2].astype(jnp.float32), middle)
     marks[3] = jnp.where(valid, marks[3], -1.0)
-    weights = weights_of(table.at[0], marks, middle, (1, 2), (0, 1, 2, 3))
-    temporal(sources, weights, tiles, adding((xn, xa), (xn1, xa1)))
-    normed_conv(xn1, act, bands[1], gains[1:2], sn1, tiles, width)
-    normed_conv(xa1, act, bands[1], gains[1:2], sa1, tiles, width)
-
-    def finish(at, target, total):
-        update = (sums[:, at] + total).astype(jnp.bfloat16).astype(jnp.float32)
-        out[0, :, at] = (xs1[:, at].astype(jnp.float32) + update).astype(jnp.bfloat16)
+    weights = weights_of(table.at[0], marks, middle, (1, 2), (3,))
+    sums_n, sums_a = mix((xn, xa), partial[1:], (so,), weights, (xn1, xa1), tiles, width)
+    stages = [(xn1, sums_n, sn1, act), (xa1, sums_a, sa1, act_too)]
+    convolve(stages, bands[1], gains[1:2], tiles, width)
 
     weights = weights_of(table.at[1], marks, middle, (0,), (1, 2))
-    temporal((sn1, sa1), weights, tiles, finish)
-
-
-def last_call(where, mine, given, gains, bands, table, ss, sn, so, sa, xn, xa, xs1, sums):
-    height, columns = xn.shape
+    add_up(xs1, partial[0], (sn1, sa1), weights, out.at[0], tiles)
+
+
+def last_call(where, mine, given, gains, bands, table, ss, sn, so, sa, xn, xa, xs1, *partial):
+    height, columns = ss.shape
     tiles, width = columns // LANES - 1, gains.shape[-1]
-    plain = pltpu.VMEM((height, columns - LANES), jnp.bfloat16)
     return pl.pallas_call(
         functools.partial(last_kernel, (tiles, width)),
         out_shape=jax.ShapeDtypeStruct((1, height, columns - LANES), jnp.bfloat16),
-        in_specs=[pl.BlockSpec(memory_space=pltpu.SMEM)] + [PLACED] * 2 + [WHOLE] * 11,
+        in_specs=[pl.BlockSpec(memory_space=pltpu.SMEM)] + [PLACED] * 2 + [WHOLE] * 13,
         out_specs=WHOLE,
-        scratch_shapes=act_scratch(height, columns)
-        + [pltpu.VMEM((height, columns), jnp.bfloat16)]
-        + [plain] * 4
-        + [pltpu.SemaphoreType.DMA((3,))],
+        scratch_shapes=act_scratch(height, columns) * 7 + [pltpu.SemaphoreType.DMA((3,))],
         compiler_params=pltpu.CompilerParams(vmem_limit_bytes=GRANT),
         cost_estimate=estimate(3),
         name="last",
-    )(where, mine, given, gains, bands, table, ss, sn, so, sa, xn, xa, xs1, sums)
+    )(where, mine, given, gains, bands, table, ss, sn, so, sa, xn, xa, xs1, *partial)
 
 
 def moved(values, hops, swap=()):
@@ -437,8 +473,8 @@
     near, middle = chip < 2, (chip == 1) | (chip == 2)
     where = jnp.stack([near, middle, device % TIME_DILATION == 1]).astype(jnp.int32)
     xs = mark_frames(frames, clip_ids)
+    inner = moved(xs, [(0, 0), (1, 2), (2, 1), (3, 3)])
     outer = moved(xs, [(0, 1), (1, 0), (2, 3), (3, 2)])
-    inner = moved(xs, [(0, 0), (1, 2), (2, 1), (3, 3)])
     ss, given, bands, table = own_call(where, xs, norm_gain, space_kernel, time_kernel)
     given = moved(given, [(chip, chip) for chip in range(4)], swap=range(4))
     outer, _ = lax.optimization_barrier((outer, given))
@@ -446,11 +482,13 @@
     after = moved(inner, [(0, 2), (1, 0), (2, 3), (3, 1)])
     xn, sn, xo, so, half = next_call(where, outer, inner, norm_gain, bands, ss, given)
     mine = moved(half, [(0, 3), (1, 1), (2, 2), (3, 0)])
-    sa, xs1, sums = after_call(where, after, norm_gain, bands, table, xs, ss, sn, xo, so)
-    mine, _ = lax.optimization_barrier((mine, sums))
-    given = moved(mine, [(chip, chip) for chip in range(4)], swap=(0, 3))
+    sa, xs1, *partial = after_call(
+        where, after, norm_gain, bands, table, xs, ss, sn, xo, so
+    )
+    mine, _ = lax.optimization_barrier((mine, sa))
+    given = moved(mine, [(chip, chip) for chip in range(4)], swap=range(4))
     return last_call(
-        where, mine, given, norm_gain, bands, table, ss, sn, so, sa, xn, after, xs1, sums
+        where, mine, given, norm_gain, bands, table, ss, sn, so, sa, xn, after, xs1, *partial
     )
 
 
@@ -474,18 +512,19 @@
     )(frame, gains, bands)
 
 
-def mix_kernel(tiles, block, frame, table, *refs):
+def mix_kernel(dims, block, frame, table, *refs):
+    tiles, width = dims
     sources, result = refs[:TIME_TAPS], refs[TIME_TAPS]
     marks = [mark_of(source, tiles) for source in sources]
     entries = range(1, TIME_TAPS + 1)
     weights = marked_weights(table.at[block], marks, marks[REACH], entries)
-    temporal(sources, weights, tiles, adding([frame], [result]))
+    mix([frame], None, sources, weights, [result], tiles, width)
     result[:, lane_tile(tiles)] = frame[:, lane_tile(tiles)]
 
 
-def mix_call(block, frame, table, sources):
-    return pl.pallas_call(
-        functools.partial(mix_kernel, frame.shape[1] // LANES - 1, block),
+def mix_call(block, frame, table, sources, width):
+    return pl.pallas_call(
+        functools.partial(mix_kernel, (frame.shape[1] // LANES - 1, width), block),
         out_shape=like(frame),
         in_specs=[WHOLE] * (2 + TIME_TAPS),
         out_specs=WHOLE,
@@ -507,7 +546,7 @@
         sources = [conv]
         for _ in range(REACH):
             sources = [moved(sources[0], up)] + sources + [moved(sources[-1], down)]
-        frame = mix_call(block, frame, table, sources)
+        frame = mix_call(block, frame, table, sources, norm_gain.shape[-1])
     return frame[None, :, : frames.shape[2]]
 
 

time: 67.7 us -> 63.9 us (0.944)
  Pallas kernels: 22.3 us -> 18.9 us
  starting transfers between devices: 14.8 us -> 12.9 us
  waiting for transfers between devices: 28.3 us -> 29.8 us
    pallas_call x1, Pallas kernels: 8.53 us -> 6.44 us  [last_call(): pl.pallas_call(functools.partial(last_kernel, (tiles, width)), out_shape=...]
    ppermute x6, starting transfers between devices: 14.8 us -> 12.9 us  [moved(): return lax.ppermute(values, 'dev', pairs)]
    ppermute x6, waiting for transfers between devices: 28.3 us -> 29.8 us  [moved(): return lax.ppermute(values, 'dev', pairs)]
  transfers between devices with their start and end apart: 6 -> 6, of which waited for: 5 -> 5; matrix products, arithmetic and copies ran while one was open for 0% -> 0% of each run, Pallas kernels for 20% -> 19%
where the time goes in v4:
time: 63.9 us; the launch traced here: 63.7 us
  waiting for transfers between devices  29.8 us (47%)
  Pallas kernels  18.9 us (30%)
  starting transfers between devices  12.9 us (20%)
  local copies, waits for them, and re-layouts  1.14 us (2%)
  between operations  0.93 us (1%)
    ppermute x6, waiting for transfers between devices, moved(): return lax.ppermute(values, 'dev', pairs)  29.8 us
    ppermute x6, starting transfers between devices, moved(): return lax.ppermute(values, 'dev', pairs)  12.9 us
    pallas_call x1, Pallas kernels, after_call(): pl.pallas_call(functools.partial(after_kernel, (tiles, width)), out_shape...  7.11 us
    pallas_call x1, Pallas kernels, last_call(): pl.pallas_call(functools.partial(last_kernel, (tiles, width)), out_shape=...  6.44 us
    pallas_call x1, Pallas kernels, next_call(): pl.pallas_call(functools.partial(next_kernel, (tiles, width)), out_shape=...  2.63 us
    pallas_call x1, Pallas kernels, own_call(): pl.pallas_call(functools.partial(own_kernel, (tiles, width)), out_shape=(...  2.53 us
  transfers between devices with their start and end apart: 6, of which 5 were waited for; matrix products, arithmetic and copies ran while one was open for 0% of the time, Pallas kernels for 19%

profile of v4, /device:TPU:0, one launch (start us, length us, event | category | flops | bytes accessed | tf_op | source)
XLA Modules:
  0.0 63.7 jit_solution(16569319725374372769)
XLA Ops:
  0.0 0.0 copy-start.1
  0.7 0.0 copy-start
  0.7 1.1 %copy-done = bf16[1,48,8192]{2,1,0:T(8,128)(2,1)S(1)} copy-done((bf16[1,48,8192]{2,1,0:T(8,128)(2,1)S(1)}, bf16[1,48,8192]{2,1,0:T(8,128)(2,1)}, u32[]{:S(2)}) %copy-start) | copy-done | bytes 786456
  1.8 0.0 copy-start.2
  1.8 0.0 copy-start.3
  1.8 0.2 mark_frames.1.frame.refs_5_
  2.0 3.1 %collective-permute-start = (bf16[48,8320]{1,0:T(8,128)(2,1)S(1)}, bf16[48,8320]{1,0:T(8,128)(2,1)S(1)}, u32[]{:S(2)}, u32[]{:S(2)}) collective-permute-start(bf16[48,8320]{1,0:T(8,128)(2,1)S(1)} %mark_frames.1.frame.refs_5_), channel_id=1, source_target_pairs={{0,2},{1,3},{2,0},{3,1},{4,6},{5,7},{6,4},{7,5},{8,10},{9,11},{10,... | collective-permute-start | bytes 2396168 | tf_op jit(solution)/shard_map/ppermute | solution.py:467
  5.1 0.7 %collective-permute-start.2 = (bf16[48,8320]{1,0:T(8,128)(2,1)S(1)}, bf16[48,8320]{1,0:T(8,128)(2,1)S(1)}, u32[]{:S(2)}, u32[]{:S(2)}) collective-permute-start(bf16[48,8320]{1,0:T(8,128)(2,1)S(1)} %mark_frames.1.frame.refs_5_), channel_id=1, source_target_pairs={{0,0},{1,1},{2,4},{3,5},{4,2},{5,3},{6,6},{7,7},{8,8},{9,9},{10,12... | collective-permute-start | bytes 2396168 | tf_op jit(solution)/shard_map/ppermute | solution.py:467
  5.8 0.1 add_convert_fusion.where.refs_0_
  5.9 0.0 copy-done.1
  5.9 0.0 copy-done.2
  5.9 0.0 copy-done.3
  5.9 2.5 %own.1 = (bf16[48,8320]{1,0:T(8,128)(2,1)S(1)}, bf16[48,4224]{1,0:T(8,128)(2,1)S(1)}, bf16[2,256,384]{2,1,0:T(8,128)(2,1)S(1)}, bf16[2,7,128,128]{3,2,1,0:T(8,128)(2,1)S(1)}) custom-call(s32[3]{0:T(128)S(1)} %add_convert_fusion.where.refs_0_, bf16[48,8320]{1,0:T(8,128)(2,1)S(1)} %mark_frames.1.frame.refs_5_, f32[2,64]{1,0:T(2,128)S(1)} %copy-done.1, ...), custom_call_target="tpu_custom_call" | custom-call | flops 1000000000 | bytes 4000000 | tf_op jit(solution)/shard_map/own/pallas_call | solution.py:282
  8.4 0.1 collective-permute-start.1
  8.5 1.7 %collective-permute-done.1.refs_6_ = bf16[48,4224]{1,0:T(8,128)(2,1)S(1)} collective-permute-done((bf16[48,4224]{1,0:T(8,128)(2,1)S(1)}, bf16[48,4224]{1,0:T(8,128)(2,1)S(1)}, u32[]{:S(2)}, u32[]{:S(2)}) %collective-permute-start.1) | collective-permute-done | bytes 405536 | tf_op jit(solution)/shard_map/ppermute | solution.py:467
  10.3 12.6 %collective-permute-done.refs_1_ = bf16[48,8320]{1,0:T(8,128)(2,1)S(1)} collective-permute-done((bf16[48,8320]{1,0:T(8,128)(2,1)S(1)}, bf16[48,8320]{1,0:T(8,128)(2,1)S(1)}, u32[]{:S(2)}, u32[]{:S(2)}) %collective-permute-start) | collective-permute-done | bytes 798752 | tf_op jit(solution)/shard_map/ppermute | solution.py:467
  22.9 0.0 collective-permute-done.2.refs_2_
  22.9 5.9 %collective-permute-start.4 = (bf16[48,8320]{1,0:T(8,128)(2,1)S(1)}, bf16[48,8320]{1,0:T(8,128)(2,1)S(1)}, u32[]{:S(2)}, u32[]{:S(2)}) collective-permute-start(bf16[48,8320]{1,0:T(8,128)(2,1)S(1)} %collective-permute-done.2.refs_2_), channel_id=1, source_target_pairs={{0,4},{1,5},{2,0},{3,1},{4,6},{5,7},{6,2},{7,3},{8,12},{9,13},{10,... | collective-permute-start | bytes 2396168 | tf_op jit(solution)/shard_map/ppermute | solution.py:467
  28.8 2.6 %next.1 = (bf16[48,8320]{1,0:T(8,128)(2,1)S(1)}, bf16[48,8320]{1,0:T(8,128)(2,1)S(1)}, bf16[48,8320]{1,0:T(8,128)(2,1)S(1)}, bf16[48,8320]{1,0:T(8,128)(2,1)S(1)}, bf16[48,4224]{1,0:T(8,128)(2,1)S(1)}) custom-call(s32[3]{0:T(128)S(1)} %add_convert_fusion.where.refs_0_, bf16[48,8320]{1,0:T(8,128)(2,1)S(1)} %collective-permute-done.refs_1_, ...), custom_call_target="tpu_custom_call" | custom-call | flops 2000000000 | bytes 8000000 | tf_op jit(solution)/shard_map/next/pallas_call | solution.py:333
  31.5 3.1 %collective-permute-start.3 = (bf16[48,4224]{1,0:T(8,128)(2,1)S(1)}, bf16[48,4224]{1,0:T(8,128)(2,1)S(1)}, u32[]{:S(2)}, u32[]{:S(2)}) collective-permute-start(bf16[48,4224]{1,0:T(8,128)(2,1)S(1)} %get-tuple-element.27), channel_id=1, source_target_pairs={{0,6},{1,7},{2,2},{3,3},{4,4},{5,5},{6,0},{7,1},{8,14},{9,15},{10,... | collective-permute-start | bytes 1216520 | tf_op jit(solution)/shard_map/ppermute | solution.py:467
  34.6 12.5 %collective-permute-done.4.refs_1_.refs_11_ = bf16[48,8320]{1,0:T(8,128)(2,1)S(1)} collective-permute-done((bf16[48,8320]{1,0:T(8,128)(2,1)S(1)}, bf16[48,8320]{1,0:T(8,128)(2,1)S(1)}, u32[]{:S(2)}, u32[]{:S(2)}) %collective-permute-start.4) | collective-permute-done | bytes 798752 | tf_op jit(solution)/shard_map/ppermute | solution.py:467
  47.0 7.1 %after.1 = (bf16[48,8320]{1,0:T(8,128)(2,1)S(1)}, bf16[48,8320]{1,0:T(8,128)(2,1)S(1)}, f32[48,8192]{1,0:T(8,128)S(1)}, f32[48,8192]{1,0:T(8,128)S(1)}, f32[48,8192]{1,0:T(8,128)S(1)}) custom-call(s32[3]{0:T(128)S(1)} %add_convert_fusion.where.refs_0_, bf16[48,8320]{1,0:T(8,128)(2,1)S(1)} %collective-permute-done.4.refs_1_.refs_11_, f32[2,64]{1,0:T(2,128)S(1)} %copy-done.1, ...), custom_call_target="tpu_custom_call" | custom-call | flops 2000000000 | bytes 8000000 | tf_op jit(solution)/shard_map/after/pallas_call | solution.py:397
  54.1 1.2 %collective-permute-done.3.refs_1_ = bf16[48,4224]{1,0:T(8,128)(2,1)S(1)} collective-permute-done((bf16[48,4224]{1,0:T(8,128)(2,1)S(1)}, bf16[48,4224]{1,0:T(8,128)(2,1)S(1)}, u32[]{:S(2)}, u32[]{:S(2)}) %collective-permute-start.3) | collective-permute-done | bytes 405536 | tf_op jit(solution)/shard_map/ppermute | solution.py:467
  55.4 0.0 collective-permute-start.5
  55.4 1.7 %collective-permute-done.5.refs_2_ = bf16[48,4224]{1,0:T(8,128)(2,1)S(1)} collective-permute-done((bf16[48,4224]{1,0:T(8,128)(2,1)S(1)}, bf16[48,4224]{1,0:T(8,128)(2,1)S(1)}, u32[]{:S(2)}, u32[]{:S(2)}) %collective-permute-start.5) | collective-permute-done | bytes 405536 | tf_op jit(solution)/shard_map/ppermute | solution.py:467
  57.1 6.4 %last.1 = bf16[1,48,8192]{2,1,0:T(8,128)(2,1)} custom-call(s32[3]{0:T(128)S(1)} %add_convert_fusion.where.refs_0_, bf16[48,4224]{1,0:T(8,128)(2,1)S(1)} %collective-permute-done.3.refs_1_, bf16[48,4224]{1,0:T(8,128)(2,1)S(1)} %collective-permute-done.5.refs_2_, f32[2,64]{1,0:T(2,128)S(1)} %copy-done.1, ...), custom_call_target="tpu_custom_call" | custom-call | flops 3000000000 | bytes 12000000 | tf_op jit(solution)/shard_map/last/pallas_call | solution.py:449
Async XLA Ops:
  0.0 5.9 %copy-start.1 = (f32[2,64]{1,0:T(2,128)S(1)}, f32[2,64]{1,0:T(2,128)}, u32[]{:S(2)}) copy-start(f32[2,64]{1,0:T(2,128)} %refs_3_.3) | copy-start | bytes 1540
  0.7 1.1 %copy-start = (bf16[1,48,8192]{2,1,0:T(8,128)(2,1)S(1)}, bf16[1,48,8192]{2,1,0:T(8,128)(2,1)}, u32[]{:S(2)}) copy-start(bf16[1,48,8192]{2,1,0:T(8,128)(2,1)} %frame.1) | copy-start | bytes 2359300
  1.8 4.1 %copy-start.2 = (bf16[2,3,3,64,64]{4,3,2,1,0:T(8,128)(2,1)S(1)}, bf16[2,3,3,64,64]{4,3,2,1,0:T(8,128)(2,1)}, u32[]{:S(2)}) copy-start(bf16[2,3,3,64,64]{4,3,2,1,0:T(8,128)(2,1)} %space.1) | copy-start | bytes 442372
  1.8 4.1 %copy-start.3 = (bf16[2,5,64,64]{3,2,1,0:T(8,128)(2,1)S(1)}, bf16[2,5,64,64]{3,2,1,0:T(8,128)(2,1)}, u32[]{:S(2)}) copy-start(bf16[2,5,64,64]{3,2,1,0:T(8,128)(2,1)} %time.1) | copy-start | bytes 245764
  2.0 20.9 %collective-permute-start = (bf16[48,8320]{1,0:T(8,128)(2,1)S(1)}, bf16[48,8320]{1,0:T(8,128)(2,1)S(1)}, u32[]{:S(2)}, u32[]{:S(2)}) collective-permute-start(bf16[48,8320]{1,0:T(8,128)(2,1)S(1)} %mark_frames.1.frame.refs_5_), channel_id=1, source_target_pairs={{0,2},{1,3},{2,0},{3,1},{4,6},{5,7},{6,4},{7,5},{8,10},{9,11},{10,... | collective-permute-start | bytes 2396168 | tf_op jit(solution)/shard_map/ppermute | solution.py:467
  5.1 17.8 %collective-permute-start.2 = (bf16[48,8320]{1,0:T(8,128)(2,1)S(1)}, bf16[48,8320]{1,0:T(8,128)(2,1)S(1)}, u32[]{:S(2)}, u32[]{:S(2)}) collective-permute-start(bf16[48,8320]{1,0:T(8,128)(2,1)S(1)} %mark_frames.1.frame.refs_5_), channel_id=1, source_target_pairs={{0,0},{1,1},{2,4},{3,5},{4,2},{5,3},{6,6},{7,7},{8,8},{9,9},{10,12... | collective-permute-start | bytes 2396168 | tf_op jit(solution)/shard_map/ppermute | solution.py:467
  8.4 1.8 %collective-permute-start.1 = (bf16[48,4224]{1,0:T(8,128)(2,1)S(1)}, bf16[48,4224]{1,0:T(8,128)(2,1)S(1)}, u32[]{:S(2)}, u32[]{:S(2)}) collective-permute-start(bf16[48,4224]{1,0:T(8,128)(2,1)S(1)} %get-tuple-element.22), channel_id=1, source_target_pairs={{0,1},{1,0},{2,3},{3,2},{4,5},{5,4},{6,7},{7,6},{8,9},{9,8},{10,11... | collective-permute-start | bytes 1216520 | tf_op jit(solution)/shard_map/ppermute | solution.py:467
  22.9 24.1 %collective-permute-start.4 = (bf16[48,8320]{1,0:T(8,128)(2,1)S(1)}, bf16[48,8320]{1,0:T(8,128)(2,1)S(1)}, u32[]{:S(2)}, u32[]{:S(2)}) collective-permute-start(bf16[48,8320]{1,0:T(8,128)(2,1)S(1)} %collective-permute-done.2.refs_2_), channel_id=1, source_target_pairs={{0,4},{1,5},{2,0},{3,1},{4,6},{5,7},{6,2},{7,3},{8,12},{9,13},{10,... | collective-permute-start | bytes 2396168 | tf_op jit(solution)/shard_map/ppermute | solution.py:467
  31.5 23.9 %collective-permute-start.3 = (bf16[48,4224]{1,0:T(8,128)(2,1)S(1)}, bf16[48,4224]{1,0:T(8,128)(2,1)S(1)}, u32[]{:S(2)}, u32[]{:S(2)}) collective-permute-start(bf16[48,4224]{1,0:T(8,128)(2,1)S(1)} %get-tuple-element.27), channel_id=1, source_target_pairs={{0,6},{1,7},{2,2},{3,3},{4,4},{5,5},{6,0},{7,1},{8,14},{9,15},{10,... | collective-permute-start | bytes 1216520 | tf_op jit(solution)/shard_map/ppermute | solution.py:467
  55.4 1.7 %collective-permute-start.5 = (bf16[48,4224]{1,0:T(8,128)(2,1)S(1)}, bf16[48,4224]{1,0:T(8,128)(2,1)S(1)}, u32[]{:S(2)}, u32[]{:S(2)}) collective-permute-start(bf16[48,4224]{1,0:T(8,128)(2,1)S(1)} %collective-permute-done.3.refs_1_), channel_id=1, source_target_pairs={{0,1},{1,0},{2,3},{3,2},{4,5},{5,4},{6,7},{7,6},{8,9},{9,8},{10,11... | collective-permute-start | bytes 1216520 | tf_op jit(solution)/shard_map/ppermute | solution.py:467

commit v5 on v4

--- a/solution.py
+++ b/solution.py
@@ -74,49 +74,40 @@
 
 def convolve(stages, bands, gain, tiles, width):
     height = stages[0][2].shape[0]
-    pack = tiles
     entries = height * tiles * LANES // GROUPS
     row = lax.broadcasted_iota(jnp.int32, (height, LANES), 0)
     lane = lax.broadcasted_iota(jnp.int32, (height, LANES), 1)
 
-    def activate(stage, first, last):
-        frame, (mean, scale), act = stage
-        for i in range(pack):
-            at = lane_tile(first * pack + i)
+    def activate(frame, scaled, act):
+        mean, scale = scaled
+        last = jnp.zeros((height, LANES), jnp.float32)
+        for i in range(tiles):
+            at = lane_tile(i)
             half = (frame[:, at].astype(jnp.float32) - mean) * scale
             turned = pltpu.roll(half + half * jnp.tanh(half), width, 1)
             act[:, at] = jnp.where(lane < width, last, turned).astype(jnp.bfloat16)
             last = turned
-        return last
-
-    def conv(act, result, first):
-        rows = [act[:, lane_tile(first * pack + i, 2)] for i in range(pack)]
+        act[:, lane_tile(tiles)] = jnp.where(lane < width, last, 0.0).astype(jnp.bfloat16)
+
+    def conv(act, result):
+        rows = [act[:, lane_tile(i, 2)] for i in range(tiles)]
         total = jnp.dot(jnp.concatenate(rows, 0), bands, preferred_element_type=jnp.float32)
-        for i in range(pack):
+        for i in range(tiles):
             part = total[i * height : (i + 1) * height]
             above = jnp.where(row == 0, 0.0, pltpu.roll(part[:, :LANES], 1, 0))
             below = pltpu.roll(part[:, 2 * LANES :], height - 1, 0)
             below = jnp.where(row == height - 1, 0.0, below)
             sums = above + part[:, LANES : 2 * LANES] + below
-            result[:, lane_tile(first * pack + i)] = sums.astype(jnp.bfloat16)
+            result[:, lane_tile(i)] = sums.astype(jnp.bfloat16)
 
     before = None
-    for stage in [*stages, None]:
-        now = None
-        if stage is not None:
-            frame, sums, result, act = stage
-            now = frame, scaling(sums, gain, entries, width), act
-
-        def block(first, last, now=now, before=before):
-            if before is not None:
-                conv(*before, first)
-            return last if now is None else activate(now, first, last)
-
-        last = lax.fori_loop(0, tiles // pack, block, jnp.zeros((height, LANES), jnp.float32))
-        before = None
-        if stage is not None:
-            act[:, lane_tile(tiles)] = jnp.where(lane < width, last, 0.0).astype(jnp.bfloat16)
-            before = act, result
+    for frame, sums, result, act in stages:
+        scaled = scaling(sums, gain, entries, width)
+        if before is not None:
+            conv(*before)
+        activate(frame, scaled, act)
+        before = act, result
+    conv(*before)
 
 
 def normed_conv(frame, act, bands, gain, result, tiles, width):
@@ -125,21 +116,15 @@
 
 def temporal(sources, weights, tiles, emit, carry=0):
     height = sources[0].shape[0]
-    pack = tiles
-
-    def block(first, carry):
-        rows = [
-            jnp.concatenate([source[:, lane_tile(first * pack + i)] for source in sources], 1)
-            for i in range(pack)
-        ]
-        total = jnp.dot(jnp.concatenate(rows, 0), weights, preferred_element_type=jnp.float32)
-        for i in range(pack):
-            part = total[i * height : (i + 1) * height]
-            sums = [part[:, at : at + LANES] for at in range(0, weights.shape[1], LANES)]
-            carry = emit(carry, first, i, lane_tile(first * pack + i), sums)
-        return carry
-
-    return lax.fori_loop(0, tiles // pack, block, carry)
+    rows = [
+        jnp.concatenate([source[:, lane_tile(i)] for source in sources], 1) for i in range(tiles)
+    ]
+    total = jnp.dot(jnp.concatenate(rows, 0), weights, preferred_element_type=jnp.float32)
+    for i in range(tiles):
+        part = total[i * height : (i + 1) * height]
+        sums = [part[:, at : at + LANES] for at in range(0, weights.shape[1], LANES)]
+        carry = emit(carry, i, sums)
+    return carry
 
 
 def rounded(start, update):
@@ -148,7 +133,8 @@
 
 
 def keep(sources, weights, results, tiles):
-    def emit(carry, first, i, at, sums):
+    def emit(carry, i, sums):
+        at = lane_tile(i)
         for result, total in zip(results, sums):
             result[:, at] = total
         return carry
@@ -156,16 +142,28 @@
     temporal(sources, weights, tiles, emit)
 
 
-def add_up(start, partial, sources, weights, result, tiles):
-    def emit(carry, first, i, at, sums):
-        result[:, at] = rounded(start[:, at], partial[:, at] + sums[0])
+def add_up(start, partial, sources, weights, held, result, sems, tiles):
+    part = tiles // 4
+    copies = []
+
+    def emit(carry, i, sums):
+        at = lane_tile(i)
+        held[:, at] = rounded(start[:, at], partial[:, at] + sums[0])
+        if i % part == part - 1:
+            columns = pl.ds((i + 1 - part) * LANES, part * LANES)
+            copy = held.at[:, columns], result.at[:, columns], sems.at[i // part]
+            copies.append(pltpu.make_async_copy(*copy))
+            copies[-1].start()
         return carry
 
     temporal(sources, weights, tiles, emit)
+    for copy in copies:
+        copy.wait()
 
 
 def mix(starts, partials, sources, weights, results, tiles, width):
-    def emit(carry, first, i, at, sums):
+    def emit(carry, i, sums):
+        at = lane_tile(i)
         after = []
         for place, (pivot, *totals) in enumerate(carry):
             update = sums[place] if partials is None else sums[place] + partials[place][:, at]
@@ -173,7 +171,7 @@
             results[place][:, at] = added
             added = added.astype(jnp.float32)
             if i == 0:
-                pivot = jnp.where(first == 0, pivot_of(added, width), pivot)
+                pivot = pivot_of(added, width)
             after.append((pivot, *gathered(added, pivot, totals)))
         return after
 
@@ -440,7 +438,7 @@
     convolve(stages, bands[1], gains[1:2], tiles, width)
 
     weights = weights_of(table.at[1], marks, middle, (0,), (1, 2))
-    add_up(xs1, partial[0], (sn1, sa1), weights, out.at[0], tiles)
+    add_up(xs1, partial[0], (sn1, sa1), weights, act, out.at[0], sem, tiles)
 
 
 def last_call(where, mine, given, gains, bands, table, ss, sn, so, sa, xn, xa, xs1, *partial):
@@ -450,8 +448,8 @@
         functools.partial(last_kernel, (tiles, width)),
         out_shape=jax.ShapeDtypeStruct((1, height, columns - LANES), jnp.bfloat16),
         in_specs=[pl.BlockSpec(memory_space=pltpu.SMEM)] + [PLACED] * 2 + [WHOLE] * 13,
-        out_specs=WHOLE,
-        scratch_shapes=act_scratch(height, columns) * 7 + [pltpu.SemaphoreType.DMA((3,))],
+        out_specs=pl.BlockSpec(memory_space=pltpu.HBM),
+        scratch_shapes=act_scratch(height, columns) * 7 + [pltpu.SemaphoreType.DMA((4,))],
         compiler_params=pltpu.CompilerParams(vmem_limit_bytes=GRANT),
         cost_estimate=estimate(3),
         name="last",
@@ -478,7 +476,7 @@
     ss, given, bands, table = own_call(where, xs, norm_gain, space_kernel, time_kernel)
     given = moved(given, [(chip, chip) for chip in range(4)], swap=range(4))
     outer, _ = lax.optimization_barrier((outer, given))
-    inner, _ = lax.optimization_barrier((inner, outer))
+    inner, _ = lax.optimization_barrier((inner, given))
     after = moved(inner, [(0, 2), (1, 0), (2, 3), (3, 1)])
     xn, sn, xo, so, half = next_call(where, outer, inner, norm_gain, bands, ss, given)
     mine = moved(half, [(0, 3), (1, 1), (2, 2), (3, 0)])

time: 63.9 us -> 64.9 us (1.016)
  starting transfers between devices: 12.9 us -> 26.1 us
  waiting for transfers between devices: 29.8 us -> 17.8 us
    ppermute x6, starting transfers between devices: 12.9 us -> 26.1 us  [moved(): return lax.ppermute(values, 'dev', pairs)]
    ppermute x6, waiting for transfers between devices: 29.8 us -> 17.8 us  [moved(): return lax.ppermute(values, 'dev', pairs)]
  transfers between devices with their start and end apart: 6 -> 6, of which waited for: 5 -> 4; matrix products, arithmetic and copies ran while one was open for 0% -> 0% of each run, Pallas kernels for 19% -> 19%
where the time goes in v5:
time: 64.9 us; the launch traced here: 64.7 us
  starting transfers between devices  26.1 us (40%)
  Pallas kernels  18.7 us (29%)
  waiting for transfers between devices  17.8 us (27%)
  local copies, waits for them, and re-layouts  1.14 us (2%)
  between operations  0.92 us (1%)
    ppermute x6, starting transfers between devices, moved(): return lax.ppermute(values, 'dev', pairs)  26.1 us
    ppermute x6, waiting for transfers between devices, moved(): return lax.ppermute(values, 'dev', pairs)  17.8 us
    pallas_call x1, Pallas kernels, after_call(): pl.pallas_call(functools.partial(after_kernel, (tiles, width)), out_shape...  7.1 us
    pallas_call x1, Pallas kernels, last_call(): pl.pallas_call(functools.partial(last_kernel, (tiles, width)), out_shape=...  6.25 us
    pallas_call x1, Pallas kernels, next_call(): pl.pallas_call(functools.partial(next_kernel, (tiles, width)), out_shape=...  2.63 us
    pallas_call x1, Pallas kernels, own_call(): pl.pallas_call(functools.partial(own_kernel, (tiles, width)), out_shape=(...  2.53 us
  transfers between devices with their start and end apart: 6, of which 4 were waited for; matrix products, arithmetic and copies ran while one was open for 0% of the time, Pallas kernels for 19%

profile of v5, /device:TPU:0, one launch (start us, length us, event | category | flops | bytes accessed | tf_op | source)
XLA Modules:
  0.0 64.7 jit_solution(2037598940333250616)
XLA Ops:
  0.0 0.0 copy-start.1
  0.7 0.0 copy-start
  0.7 1.1 %copy-done = bf16[1,48,8192]{2,1,0:T(8,128)(2,1)S(1)} copy-done((bf16[1,48,8192]{2,1,0:T(8,128)(2,1)S(1)}, bf16[1,48,8192]{2,1,0:T(8,128)(2,1)}, u32[]{:S(2)}) %copy-start) | copy-done | bytes 786456
  1.8 0.0 copy-start.2
  1.8 0.0 copy-start.3
  1.8 0.2 mark_frames.1.frame.refs_5_
  2.0 0.7 %collective-permute-start.2 = (bf16[48,8320]{1,0:T(8,128)(2,1)S(1)}, bf16[48,8320]{1,0:T(8,128)(2,1)S(1)}, u32[]{:S(2)}, u32[]{:S(2)}) collective-permute-start(bf16[48,8320]{1,0:T(8,128)(2,1)S(1)} %mark_frames.1.frame.refs_5_), channel_id=1, source_target_pairs={{0,0},{1,1},{2,4},{3,5},{4,2},{5,3},{6,6},{7,7},{8,8},{9,9},{10,12... | collective-permute-start | bytes 2396168 | tf_op jit(solution)/shard_map/ppermute | solution.py:465
  2.7 0.1 add_convert_fusion.where.refs_0_
  2.8 0.0 copy-done.1
  2.8 0.0 copy-done.2
  2.8 0.0 copy-done.3
  2.8 2.5 %own.1 = (bf16[48,8320]{1,0:T(8,128)(2,1)S(1)}, bf16[48,4224]{1,0:T(8,128)(2,1)S(1)}, bf16[2,256,384]{2,1,0:T(8,128)(2,1)S(1)}, bf16[2,7,128,128]{3,2,1,0:T(8,128)(2,1)S(1)}) custom-call(s32[3]{0:T(128)S(1)} %add_convert_fusion.where.refs_0_, bf16[48,8320]{1,0:T(8,128)(2,1)S(1)} %mark_frames.1.frame.refs_5_, f32[2,64]{1,0:T(2,128)S(1)} %copy-done.1, ...), custom_call_target="tpu_custom_call" | custom-call | flops 1000000000 | bytes 4000000 | tf_op jit(solution)/shard_map/own/pallas_call | solution.py:280
  5.3 0.6 collective-permute-start.1
  5.9 5.4 %collective-permute-start = (bf16[48,8320]{1,0:T(8,128)(2,1)S(1)}, bf16[48,8320]{1,0:T(8,128)(2,1)S(1)}, u32[]{:S(2)}, u32[]{:S(2)}) collective-permute-start(bf16[48,8320]{1,0:T(8,128)(2,1)S(1)} %mark_frames.1.frame.refs_5_), channel_id=1, source_target_pairs={{0,2},{1,3},{2,0},{3,1},{4,6},{5,7},{6,4},{7,5},{8,10},{9,11},{10,... | collective-permute-start | bytes 2396168 | tf_op jit(solution)/shard_map/ppermute | solution.py:465
  11.3 0.0 collective-permute-done.1.refs_6_
  11.3 0.0 collective-permute-done.2.refs_2_
  11.3 16.2 %collective-permute-start.4 = (bf16[48,8320]{1,0:T(8,128)(2,1)S(1)}, bf16[48,8320]{1,0:T(8,128)(2,1)S(1)}, u32[]{:S(2)}, u32[]{:S(2)}) collective-permute-start(bf16[48,8320]{1,0:T(8,128)(2,1)S(1)} %collective-permute-done.2.refs_2_), channel_id=1, source_target_pairs={{0,4},{1,5},{2,0},{3,1},{4,6},{5,7},{6,2},{7,3},{8,12},{9,13},{10,... | collective-permute-start | bytes 2396168 | tf_op jit(solution)/shard_map/ppermute | solution.py:465
  27.5 2.5 %collective-permute-done.refs_1_ = bf16[48,8320]{1,0:T(8,128)(2,1)S(1)} collective-permute-done((bf16[48,8320]{1,0:T(8,128)(2,1)S(1)}, bf16[48,8320]{1,0:T(8,128)(2,1)S(1)}, u32[]{:S(2)}, u32[]{:S(2)}) %collective-permute-start) | collective-permute-done | bytes 798752 | tf_op jit(solution)/shard_map/ppermute | solution.py:465
  30.0 2.6 %next.1 = (bf16[48,8320]{1,0:T(8,128)(2,1)S(1)}, bf16[48,8320]{1,0:T(8,128)(2,1)S(1)}, bf16[48,8320]{1,0:T(8,128)(2,1)S(1)}, bf16[48,8320]{1,0:T(8,128)(2,1)S(1)}, bf16[48,4224]{1,0:T(8,128)(2,1)S(1)}) custom-call(s32[3]{0:T(128)S(1)} %add_convert_fusion.where.refs_0_, bf16[48,8320]{1,0:T(8,128)(2,1)S(1)} %collective-permute-done.refs_1_, ...), custom_call_target="tpu_custom_call" | custom-call | flops 2000000000 | bytes 8000000 | tf_op jit(solution)/shard_map/next/pallas_call | solution.py:331
  32.6 3.2 %collective-permute-start.3 = (bf16[48,4224]{1,0:T(8,128)(2,1)S(1)}, bf16[48,4224]{1,0:T(8,128)(2,1)S(1)}, u32[]{:S(2)}, u32[]{:S(2)}) collective-permute-start(bf16[48,4224]{1,0:T(8,128)(2,1)S(1)} %get-tuple-element.27), channel_id=1, source_target_pairs={{0,6},{1,7},{2,2},{3,3},{4,4},{5,5},{6,0},{7,1},{8,14},{9,15},{10,... | collective-permute-start | bytes 1216520 | tf_op jit(solution)/shard_map/ppermute | solution.py:465
  35.9 11.0 %collective-permute-done.4.refs_1_.refs_11_ = bf16[48,8320]{1,0:T(8,128)(2,1)S(1)} collective-permute-done((bf16[48,8320]{1,0:T(8,128)(2,1)S(1)}, bf16[48,8320]{1,0:T(8,128)(2,1)S(1)}, u32[]{:S(2)}, u32[]{:S(2)}) %collective-permute-start.4) | collective-permute-done | bytes 798752 | tf_op jit(solution)/shard_map/ppermute | solution.py:465
  46.8 7.1 %after.1 = (bf16[48,8320]{1,0:T(8,128)(2,1)S(1)}, bf16[48,8320]{1,0:T(8,128)(2,1)S(1)}, f32[48,8192]{1,0:T(8,128)S(1)}, f32[48,8192]{1,0:T(8,128)S(1)}, f32[48,8192]{1,0:T(8,128)S(1)}) custom-call(s32[3]{0:T(128)S(1)} %add_convert_fusion.where.refs_0_, bf16[48,8320]{1,0:T(8,128)(2,1)S(1)} %collective-permute-done.4.refs_1_.refs_11_, f32[2,64]{1,0:T(2,128)S(1)} %copy-done.1, ...), custom_call_target="tpu_custom_call" | custom-call | flops 2000000000 | bytes 8000000 | tf_op jit(solution)/shard_map/after/pallas_call | solution.py:395
  53.9 2.6 %collective-permute-done.3.refs_1_ = bf16[48,4224]{1,0:T(8,128)(2,1)S(1)} collective-permute-done((bf16[48,4224]{1,0:T(8,128)(2,1)S(1)}, bf16[48,4224]{1,0:T(8,128)(2,1)S(1)}, u32[]{:S(2)}, u32[]{:S(2)}) %collective-permute-start.3) | collective-permute-done | bytes 405536 | tf_op jit(solution)/shard_map/ppermute | solution.py:465
  56.6 0.0 collective-permute-start.5
  56.6 1.7 %collective-permute-done.5.refs_2_ = bf16[48,4224]{1,0:T(8,128)(2,1)S(1)} collective-permute-done((bf16[48,4224]{1,0:T(8,128)(2,1)S(1)}, bf16[48,4224]{1,0:T(8,128)(2,1)S(1)}, u32[]{:S(2)}, u32[]{:S(2)}) %collective-permute-start.5) | collective-permute-done | bytes 405536 | tf_op jit(solution)/shard_map/ppermute | solution.py:465
  58.3 6.2 %last.1 = bf16[1,48,8192]{2,1,0:T(8,128)(2,1)} custom-call(s32[3]{0:T(128)S(1)} %add_convert_fusion.where.refs_0_, bf16[48,4224]{1,0:T(8,128)(2,1)S(1)} %collective-permute-done.3.refs_1_, bf16[48,4224]{1,0:T(8,128)(2,1)S(1)} %collective-permute-done.5.refs_2_, f32[2,64]{1,0:T(2,128)S(1)} %copy-done.1, ...), custom_call_target="tpu_custom_call" | custom-call | flops 3000000000 | bytes 12000000 | tf_op jit(solution)/shard_map/last/pallas_call | solution.py:447
Async XLA Ops:
  0.0 2.8 %copy-start.1 = (f32[2,64]{1,0:T(2,128)S(1)}, f32[2,64]{1,0:T(2,128)}, u32[]{:S(2)}) copy-start(f32[2,64]{1,0:T(2,128)} %refs_3_.3) | copy-start | bytes 1540
  0.7 1.1 %copy-start = (bf16[1,48,8192]{2,1,0:T(8,128)(2,1)S(1)}, bf16[1,48,8192]{2,1,0:T(8,128)(2,1)}, u32[]{:S(2)}) copy-start(bf16[1,48,8192]{2,1,0:T(8,128)(2,1)} %frame.1) | copy-start | bytes 2359300
  1.8 1.0 %copy-start.2 = (bf16[2,3,3,64,64]{4,3,2,1,0:T(8,128)(2,1)S(1)}, bf16[2,3,3,64,64]{4,3,2,1,0:T(8,128)(2,1)}, u32[]{:S(2)}) copy-start(bf16[2,3,3,64,64]{4,3,2,1,0:T(8,128)(2,1)} %space.1) | copy-start | bytes 442372
  1.8 1.0 %copy-start.3 = (bf16[2,5,64,64]{3,2,1,0:T(8,128)(2,1)S(1)}, bf16[2,5,64,64]{3,2,1,0:T(8,128)(2,1)}, u32[]{:S(2)}) copy-start(bf16[2,5,64,64]{3,2,1,0:T(8,128)(2,1)} %time.1) | copy-start | bytes 245764
  2.0 9.3 %collective-permute-start.2 = (bf16[48,8320]{1,0:T(8,128)(2,1)S(1)}, bf16[48,8320]{1,0:T(8,128)(2,1)S(1)}, u32[]{:S(2)}, u32[]{:S(2)}) collective-permute-start(bf16[48,8320]{1,0:T(8,128)(2,1)S(1)} %mark_frames.1.frame.refs_5_), channel_id=1, source_target_pairs={{0,0},{1,1},{2,4},{3,5},{4,2},{5,3},{6,6},{7,7},{8,8},{9,9},{10,12... | collective-permute-start | bytes 2396168 | tf_op jit(solution)/shard_map/ppermute | solution.py:465
  5.3 6.0 %collective-permute-start.1 = (bf16[48,4224]{1,0:T(8,128)(2,1)S(1)}, bf16[48,4224]{1,0:T(8,128)(2,1)S(1)}, u32[]{:S(2)}, u32[]{:S(2)}) collective-permute-start(bf16[48,4224]{1,0:T(8,128)(2,1)S(1)} %get-tuple-element.22), channel_id=1, source_target_pairs={{0,1},{1,0},{2,3},{3,2},{4,5},{5,4},{6,7},{7,6},{8,9},{9,8},{10,11... | collective-permute-start | bytes 1216520 | tf_op jit(solution)/shard_map/ppermute | solution.py:465
  5.9 24.1 %collective-permute-start = (bf16[48,8320]{1,0:T(8,128)(2,1)S(1)}, bf16[48,8320]{1,0:T(8,128)(2,1)S(1)}, u32[]{:S(2)}, u32[]{:S(2)}) collective-permute-start(bf16[48,8320]{1,0:T(8,128)(2,1)S(1)} %mark_frames.1.frame.refs_5_), channel_id=1, source_target_pairs={{0,2},{1,3},{2,0},{3,1},{4,6},{5,7},{6,4},{7,5},{8,10},{9,11},{10,... | collective-permute-start | bytes 2396168 | tf_op jit(solution)/shard_map/ppermute | solution.py:465
  11.3 35.5 %collective-permute-start.4 = (bf16[48,8320]{1,0:T(8,128)(2,1)S(1)}, bf16[48,8320]{1,0:T(8,128)(2,1)S(1)}, u32[]{:S(2)}, u32[]{:S(2)}) collective-permute-start(bf16[48,8320]{1,0:T(8,128)(2,1)S(1)} %collective-permute-done.2.refs_2_), channel_id=1, source_target_pairs={{0,4},{1,5},{2,0},{3,1},{4,6},{5,7},{6,2},{7,3},{8,12},{9,13},{10,... | collective-permute-start | bytes 2396168 | tf_op jit(solution)/shard_map/ppermute | solution.py:465
  32.6 24.0 %collective-permute-start.3 = (bf16[48,4224]{1,0:T(8,128)(2,1)S(1)}, bf16[48,4224]{1,0:T(8,128)(2,1)S(1)}, u32[]{:S(2)}, u32[]{:S(2)}) collective-permute-start(bf16[48,4224]{1,0:T(8,128)(2,1)S(1)} %get-tuple-element.27), channel_id=1, source_target_pairs={{0,6},{1,7},{2,2},{3,3},{4,4},{5,5},{6,0},{7,1},{8,14},{9,15},{10,... | collective-permute-start | bytes 1216520 | tf_op jit(solution)/shard_map/ppermute | solution.py:465
  56.6 1.7 %collective-permute-start.5 = (bf16[48,4224]{1,0:T(8,128)(2,1)S(1)}, bf16[48,4224]{1,0:T(8,128)(2,1)S(1)}, u32[]{:S(2)}, u32[]{:S(2)}) collective-permute-start(bf16[48,4224]{1,0:T(8,128)(2,1)S(1)} %collective-permute-done.3.refs_1_), channel_id=1, source_target_pairs={{0,1},{1,0},{2,3},{3,2},{4,5},{5,4},{6,7},{7,6},{8,9},{9,8},{10,11... | collective-permute-start | bytes 1216520 | tf_op jit(solution)/shard_map/ppermute | solution.py:465

commit v6 on v5

--- a/solution.py
+++ b/solution.py
@@ -198,11 +198,14 @@
     copy.wait()
 
 
-def mark_kernel(ids, frame, marked, sem):
+def mark_kernel(ids, frame, marked, held, sem, id_sem):
     columns = frame.shape[-1]
+    id_copy = pltpu.make_async_copy(ids, held, id_sem)
+    id_copy.start()
     copy = pltpu.make_async_copy(frame.at[0], marked.at[:, pl.ds(0, columns)], sem)
     copy.start()
-    mark = jnp.broadcast_to(ids[...].astype(jnp.float32), (marked.shape[0], LANES))
+    id_copy.wait()
+    mark = jnp.full((marked.shape[0], LANES), held[0].astype(jnp.float32))
     marked[:, columns:] = mark.astype(jnp.bfloat16)
     copy.wait()
 
@@ -212,12 +215,12 @@
     return pl.pallas_call(
         mark_kernel,
         out_shape=jax.ShapeDtypeStruct((height, columns + LANES), frames.dtype),
-        in_specs=[WHOLE, PLACED],
+        in_specs=[pl.BlockSpec(memory_space=pltpu.HBM), PLACED],
         out_specs=WHOLE,
-        scratch_shapes=[pltpu.SemaphoreType.DMA],
+        scratch_shapes=[pltpu.SMEM((1,), jnp.int32)] + [pltpu.SemaphoreType.DMA] * 2,
         compiler_params=pltpu.CompilerParams(vmem_limit_bytes=4 << 20),
         name="mark_frames",
-    )(clip_ids[:, None], frames)
+    )(clip_ids, frames)
 
 
 def build_bands(space, bands):

time: 64.9 us -> 65.3 us (level)
  no operation moved by 1% of the time
where the time goes in v6:
time: 65.3 us; the launch traced here: 65.1 us
  starting transfers between devices  26.1 us (40%)
  Pallas kernels  19.1 us (29%)
  waiting for transfers between devices  17.8 us (27%)
  local copies, waits for them, and re-layouts  1.14 us (2%)
  between operations  0.92 us (1%)
    ppermute x6, starting transfers between devices, moved(): return lax.ppermute(values, 'dev', pairs)  26.1 us
    ppermute x6, waiting for transfers between devices, moved(): return lax.ppermute(values, 'dev', pairs)  17.8 us
    pallas_call x1, Pallas kernels, after_call(): pl.pallas_call(functools.partial(after_kernel, (tiles, width)), out_shape...  7.11 us
    pallas_call x1, Pallas kernels, last_call(): pl.pallas_call(functools.partial(last_kernel, (tiles, width)), out_shape=...  6.25 us
    pallas_call x1, Pallas kernels, next_call(): pl.pallas_call(functools.partial(next_kernel, (tiles, width)), out_shape=...  2.62 us
    pallas_call x1, Pallas kernels, own_call(): pl.pallas_call(functools.partial(own_kernel, (tiles, width)), out_shape=(...  2.53 us
  transfers between devices with their start and end apart: 6, of which 4 were waited for; matrix products, arithmetic and copies ran while one was open for 0% of the time, Pallas kernels for 19%

profile of v6, /device:TPU:0, one launch (start us, length us, event | category | flops | bytes accessed | tf_op | source)
XLA Modules:
  0.0 65.1 jit_solution(1748202222948042034)
XLA Ops:
  0.0 0.0 copy-start.1
  0.7 0.0 copy-start
  0.7 1.1 %copy-done = bf16[1,48,8192]{2,1,0:T(8,128)(2,1)S(1)} copy-done((bf16[1,48,8192]{2,1,0:T(8,128)(2,1)S(1)}, bf16[1,48,8192]{2,1,0:T(8,128)(2,1)}, u32[]{:S(2)}) %copy-start) | copy-done | bytes 786456
  1.8 0.0 copy-start.2
  1.8 0.0 copy-start.3
  1.8 0.6 mark_frames.1.frame.refs_5_
  2.4 0.7 %collective-permute-start.2 = (bf16[48,8320]{1,0:T(8,128)(2,1)S(1)}, bf16[48,8320]{1,0:T(8,128)(2,1)S(1)}, u32[]{:S(2)}, u32[]{:S(2)}) collective-permute-start(bf16[48,8320]{1,0:T(8,128)(2,1)S(1)} %mark_frames.1.frame.refs_5_), channel_id=1, source_target_pairs={{0,0},{1,1},{2,4},{3,5},{4,2},{5,3},{6,6},{7,7},{8,8},{9,9},{10,12... | collective-permute-start | bytes 2396168 | tf_op jit(solution)/shard_map/ppermute | solution.py:468
  3.1 0.1 add_convert_fusion.where.refs_0_
  3.2 0.0 copy-done.1
  3.2 0.0 copy-done.2
  3.2 0.0 copy-done.3
  3.2 2.5 %own.1 = (bf16[48,8320]{1,0:T(8,128)(2,1)S(1)}, bf16[48,4224]{1,0:T(8,128)(2,1)S(1)}, bf16[2,256,384]{2,1,0:T(8,128)(2,1)S(1)}, bf16[2,7,128,128]{3,2,1,0:T(8,128)(2,1)S(1)}) custom-call(s32[3]{0:T(128)S(1)} %add_convert_fusion.where.refs_0_, bf16[48,8320]{1,0:T(8,128)(2,1)S(1)} %mark_frames.1.frame.refs_5_, f32[2,64]{1,0:T(2,128)S(1)} %copy-done.1, ...), custom_call_target="tpu_custom_call" | custom-call | flops 1000000000 | bytes 4000000 | tf_op jit(solution)/shard_map/own/pallas_call | solution.py:283
  5.8 0.6 collective-permute-start.1
  6.3 5.4 %collective-permute-start = (bf16[48,8320]{1,0:T(8,128)(2,1)S(1)}, bf16[48,8320]{1,0:T(8,128)(2,1)S(1)}, u32[]{:S(2)}, u32[]{:S(2)}) collective-permute-start(bf16[48,8320]{1,0:T(8,128)(2,1)S(1)} %mark_frames.1.frame.refs_5_), channel_id=1, source_target_pairs={{0,2},{1,3},{2,0},{3,1},{4,6},{5,7},{6,4},{7,5},{8,10},{9,11},{10,... | collective-permute-start | bytes 2396168 | tf_op jit(solution)/shard_map/ppermute | solution.py:468
  11.7 0.0 collective-permute-done.1.refs_6_
  11.7 0.0 collective-permute-done.2.refs_2_
  11.7 16.2 %collective-permute-start.4 = (bf16[48,8320]{1,0:T(8,128)(2,1)S(1)}, bf16[48,8320]{1,0:T(8,128)(2,1)S(1)}, u32[]{:S(2)}, u32[]{:S(2)}) collective-permute-start(bf16[48,8320]{1,0:T(8,128)(2,1)S(1)} %collective-permute-done.2.refs_2_), channel_id=1, source_target_pairs={{0,4},{1,5},{2,0},{3,1},{4,6},{5,7},{6,2},{7,3},{8,12},{9,13},{10,... | collective-permute-start | bytes 2396168 | tf_op jit(solution)/shard_map/ppermute | solution.py:468
  27.9 2.5 %collective-permute-done.refs_1_ = bf16[48,8320]{1,0:T(8,128)(2,1)S(1)} collective-permute-done((bf16[48,8320]{1,0:T(8,128)(2,1)S(1)}, bf16[48,8320]{1,0:T(8,128)(2,1)S(1)}, u32[]{:S(2)}, u32[]{:S(2)}) %collective-permute-start) | collective-permute-done | bytes 798752 | tf_op jit(solution)/shard_map/ppermute | solution.py:468
  30.4 2.6 %next.1 = (bf16[48,8320]{1,0:T(8,128)(2,1)S(1)}, bf16[48,8320]{1,0:T(8,128)(2,1)S(1)}, bf16[48,8320]{1,0:T(8,128)(2,1)S(1)}, bf16[48,8320]{1,0:T(8,128)(2,1)S(1)}, bf16[48,4224]{1,0:T(8,128)(2,1)S(1)}) custom-call(s32[3]{0:T(128)S(1)} %add_convert_fusion.where.refs_0_, bf16[48,8320]{1,0:T(8,128)(2,1)S(1)} %collective-permute-done.refs_1_, ...), custom_call_target="tpu_custom_call" | custom-call | flops 2000000000 | bytes 8000000 | tf_op jit(solution)/shard_map/next/pallas_call | solution.py:334
  33.0 3.3 %collective-permute-start.3 = (bf16[48,4224]{1,0:T(8,128)(2,1)S(1)}, bf16[48,4224]{1,0:T(8,128)(2,1)S(1)}, u32[]{:S(2)}, u32[]{:S(2)}) collective-permute-start(bf16[48,4224]{1,0:T(8,128)(2,1)S(1)} %get-tuple-element.27), channel_id=1, source_target_pairs={{0,6},{1,7},{2,2},{3,3},{4,4},{5,5},{6,0},{7,1},{8,14},{9,15},{10,... | collective-permute-start | bytes 1216520 | tf_op jit(solution)/shard_map/ppermute | solution.py:468
  36.3 11.0 %collective-permute-done.4.refs_1_.refs_11_ = bf16[48,8320]{1,0:T(8,128)(2,1)S(1)} collective-permute-done((bf16[48,8320]{1,0:T(8,128)(2,1)S(1)}, bf16[48,8320]{1,0:T(8,128)(2,1)S(1)}, u32[]{:S(2)}, u32[]{:S(2)}) %collective-permute-start.4) | collective-permute-done | bytes 798752 | tf_op jit(solution)/shard_map/ppermute | solution.py:468
  47.2 7.1 %after.1 = (bf16[48,8320]{1,0:T(8,128)(2,1)S(1)}, bf16[48,8320]{1,0:T(8,128)(2,1)S(1)}, f32[48,8192]{1,0:T(8,128)S(1)}, f32[48,8192]{1,0:T(8,128)S(1)}, f32[48,8192]{1,0:T(8,128)S(1)}) custom-call(s32[3]{0:T(128)S(1)} %add_convert_fusion.where.refs_0_, bf16[48,8320]{1,0:T(8,128)(2,1)S(1)} %collective-permute-done.4.refs_1_.refs_11_, f32[2,64]{1,0:T(2,128)S(1)} %copy-done.1, ...), custom_call_target="tpu_custom_call" | custom-call | flops 2000000000 | bytes 8000000 | tf_op jit(solution)/shard_map/after/pallas_call | solution.py:398
  54.3 2.6 %collective-permute-done.3.refs_1_ = bf16[48,4224]{1,0:T(8,128)(2,1)S(1)} collective-permute-done((bf16[48,4224]{1,0:T(8,128)(2,1)S(1)}, bf16[48,4224]{1,0:T(8,128)(2,1)S(1)}, u32[]{:S(2)}, u32[]{:S(2)}) %collective-permute-start.3) | collective-permute-done | bytes 405536 | tf_op jit(solution)/shard_map/ppermute | solution.py:468
  57.0 0.0 collective-permute-start.5
  57.0 1.7 %collective-permute-done.5.refs_2_ = bf16[48,4224]{1,0:T(8,128)(2,1)S(1)} collective-permute-done((bf16[48,4224]{1,0:T(8,128)(2,1)S(1)}, bf16[48,4224]{1,0:T(8,128)(2,1)S(1)}, u32[]{:S(2)}, u32[]{:S(2)}) %collective-permute-start.5) | collective-permute-done | bytes 405536 | tf_op jit(solution)/shard_map/ppermute | solution.py:468
  58.7 6.2 %last.1 = bf16[1,48,8192]{2,1,0:T(8,128)(2,1)} custom-call(s32[3]{0:T(128)S(1)} %add_convert_fusion.where.refs_0_, bf16[48,4224]{1,0:T(8,128)(2,1)S(1)} %collective-permute-done.3.refs_1_, bf16[48,4224]{1,0:T(8,128)(2,1)S(1)} %collective-permute-done.5.refs_2_, f32[2,64]{1,0:T(2,128)S(1)} %copy-done.1, ...), custom_call_target="tpu_custom_call" | custom-call | flops 3000000000 | bytes 12000000 | tf_op jit(solution)/shard_map/last/pallas_call | solution.py:450
Async XLA Ops:
  0.0 3.2 %copy-start.1 = (f32[2,64]{1,0:T(2,128)S(1)}, f32[2,64]{1,0:T(2,128)}, u32[]{:S(2)}) copy-start(f32[2,64]{1,0:T(2,128)} %refs_3_.3) | copy-start | bytes 1540
  0.7 1.1 %copy-start = (bf16[1,48,8192]{2,1,0:T(8,128)(2,1)S(1)}, bf16[1,48,8192]{2,1,0:T(8,128)(2,1)}, u32[]{:S(2)}) copy-start(bf16[1,48,8192]{2,1,0:T(8,128)(2,1)} %frame.1) | copy-start | bytes 2359300
  1.8 1.4 %copy-start.2 = (bf16[2,3,3,64,64]{4,3,2,1,0:T(8,128)(2,1)S(1)}, bf16[2,3,3,64,64]{4,3,2,1,0:T(8,128)(2,1)}, u32[]{:S(2)}) copy-start(bf16[2,3,3,64,64]{4,3,2,1,0:T(8,128)(2,1)} %space.1) | copy-start | bytes 442372
  1.8 1.4 %copy-start.3 = (bf16[2,5,64,64]{3,2,1,0:T(8,128)(2,1)S(1)}, bf16[2,5,64,64]{3,2,1,0:T(8,128)(2,1)}, u32[]{:S(2)}) copy-start(bf16[2,5,64,64]{3,2,1,0:T(8,128)(2,1)} %time.1) | copy-start | bytes 245764
  2.4 9.3 %collective-permute-start.2 = (bf16[48,8320]{1,0:T(8,128)(2,1)S(1)}, bf16[48,8320]{1,0:T(8,128)(2,1)S(1)}, u32[]{:S(2)}, u32[]{:S(2)}) collective-permute-start(bf16[48,8320]{1,0:T(8,128)(2,1)S(1)} %mark_frames.1.frame.refs_5_), channel_id=1, source_target_pairs={{0,0},{1,1},{2,4},{3,5},{4,2},{5,3},{6,6},{7,7},{8,8},{9,9},{10,12... | collective-permute-start | bytes 2396168 | tf_op jit(solution)/shard_map/ppermute | solution.py:468
  5.8 6.0 %collective-permute-start.1 = (bf16[48,4224]{1,0:T(8,128)(2,1)S(1)}, bf16[48,4224]{1,0:T(8,128)(2,1)S(1)}, u32[]{:S(2)}, u32[]{:S(2)}) collective-permute-start(bf16[48,4224]{1,0:T(8,128)(2,1)S(1)} %get-tuple-element.22), channel_id=1, source_target_pairs={{0,1},{1,0},{2,3},{3,2},{4,5},{5,4},{6,7},{7,6},{8,9},{9,8},{10,11... | collective-permute-start | bytes 1216520 | tf_op jit(solution)/shard_map/ppermute | solution.py:468
  6.3 24.1 %collective-permute-start = (bf16[48,8320]{1,0:T(8,128)(2,1)S(1)}, bf16[48,8320]{1,0:T(8,128)(2,1)S(1)}, u32[]{:S(2)}, u32[]{:S(2)}) collective-permute-start(bf16[48,8320]{1,0:T(8,128)(2,1)S(1)} %mark_frames.1.frame.refs_5_), channel_id=1, source_target_pairs={{0,2},{1,3},{2,0},{3,1},{4,6},{5,7},{6,4},{7,5},{8,10},{9,11},{10,... | collective-permute-start | bytes 2396168 | tf_op jit(solution)/shard_map/ppermute | solution.py:468
  11.7 35.5 %collective-permute-start.4 = (bf16[48,8320]{1,0:T(8,128)(2,1)S(1)}, bf16[48,8320]{1,0:T(8,128)(2,1)S(1)}, u32[]{:S(2)}, u32[]{:S(2)}) collective-permute-start(bf16[48,8320]{1,0:T(8,128)(2,1)S(1)} %collective-permute-done.2.refs_2_), channel_id=1, source_target_pairs={{0,4},{1,5},{2,0},{3,1},{4,6},{5,7},{6,2},{7,3},{8,12},{9,13},{10,... | collective-permute-start | bytes 2396168 | tf_op jit(solution)/shard_map/ppermute | solution.py:468
  33.0 24.0 %collective-permute-start.3 = (bf16[48,4224]{1,0:T(8,128)(2,1)S(1)}, bf16[48,4224]{1,0:T(8,128)(2,1)S(1)}, u32[]{:S(2)}, u32[]{:S(2)}) collective-permute-start(bf16[48,4224]{1,0:T(8,128)(2,1)S(1)} %get-tuple-element.27), channel_id=1, source_target_pairs={{0,6},{1,7},{2,2},{3,3},{4,4},{5,5},{6,0},{7,1},{8,14},{9,15},{10,... | collective-permute-start | bytes 1216520 | tf_op jit(solution)/shard_map/ppermute | solution.py:468
  57.0 1.7 %collective-permute-start.5 = (bf16[48,4224]{1,0:T(8,128)(2,1)S(1)}, bf16[48,4224]{1,0:T(8,128)(2,1)S(1)}, u32[]{:S(2)}, u32[]{:S(2)}) collective-permute-start(bf16[48,4224]{1,0:T(8,128)(2,1)S(1)} %collective-permute-done.3.refs_1_), channel_id=1, source_target_pairs={{0,1},{1,0},{2,3},{3,2},{4,5},{5,4},{6,7},{7,6},{8,9},{9,8},{10,11... | collective-permute-start | bytes 1216520 | tf_op jit(solution)/shard_map/ppermute | solution.py:468
